TPU v7x, 32 devices: a whole 2x2x4 slice. The times are simulated.
32 devices in a mesh: row: 4 (over y, x), col: 8 (over z, core).
Axes of the slice: x: 2, y: 2, z: 4, core: 2. Of those that a mesh axis runs over, the one named last changes fastest.
Arguments:
- owned_blocks: bfloat16 [1024, 8, 128, 128], P(('row', 'col')), may hold values from -0.8984375 to 0.8984375
- owned_rows: int32 [1024], P(('row', 'col')), may hold values from 0 to 64, as said below
- owned_cols: int32 [1024, 8], P(('row', 'col')), may hold values from 0 to 31
- keep: int32 [8, 256], P('row', 'col'), may hold values 0 or 1
Outputs:
- purified: bfloat16 [1024, 32768], P('row', 'col')
Inputs may be any that keep to these rules, and one draw needn't show every extreme that they name: `owned_rows`: every block row of P stands in exactly one slot, in a slot of its own band; in every band some owner fills all 8 of its slots for that band.
All inputs are finite; a program needn't handle non-finite values. No bound on the sum of `keep` on one device may be relied on, other than what follows from the above.
Results may differ from a plain program's by a relative error of at most 0.005.
Values may be sent and summed in bfloat16 or wider, within the bound.
A program may use at most 256 MiB of HBM per device.

v0:
```python
import jax
import jax.numpy as jnp
from jax import lax
from jax.sharding import PartitionSpec as P


def passed_along(value, axis, by):
    devices = lax.axis_size(axis)
    return lax.ppermute(value, axis, [(i, (i + by) % devices) for i in range(devices)])


def local(owned_blocks, owned_rows, owned_cols, keep):
    grid_rows = lax.axis_size("row")
    grid_cols = lax.axis_size("col")
    my_row = lax.axis_index("row")
    my_col = lax.axis_index("col")
    block_size = owned_blocks.shape[-1]
    slot_count = owned_rows.shape[0]
    per_band = slot_count // grid_rows
    window_rows = keep.shape[0]
    group_cols = keep.shape[1]
    band_rows = 2 * group_cols
    stacked = owned_blocks.reshape(grid_rows, per_band, grid_cols, block_size, block_size)
    local_rows = owned_rows.reshape(grid_rows, per_band)
    local_cols = owned_cols.reshape(grid_rows, per_band, grid_cols)
    dest_row = jnp.arange(grid_rows, dtype=jnp.int32)[:, None, None]
    dest_col = jnp.arange(grid_cols, dtype=jnp.int32)[None, :, None]
    slot_ids = jnp.arange(per_band, dtype=jnp.int32)[None, None, :]
    band_table = (dest_row + dest_col) % grid_rows
    outgoing = stacked[band_table, slot_ids, dest_col]
    row_labels = local_rows[band_table, slot_ids]
    col_labels = local_cols[band_table, slot_ids, dest_col]
    labels = jnp.stack([row_labels, col_labels], axis=-1)
    arrived, arrived_tags = (
        lax.all_to_all(
            outgoing.reshape(grid_rows * grid_cols, per_band, block_size, block_size),
            ("row", "col"),
            split_axis=0,
            concat_axis=0,
            tiled=True,
        ),
        lax.all_to_all(
            labels.reshape(grid_rows * grid_cols, per_band, 2),
            ("row", "col"),
            split_axis=0,
            concat_axis=0,
            tiled=True,
        ),
    )
    arrived = arrived.reshape(-1, block_size, block_size)
    arrived_tags = arrived_tags.reshape(-1, 2)
    band_blocks = (
        jnp.zeros((band_rows, block_size, block_size), owned_blocks.dtype)
        .at[arrived_tags[:, 0]]
        .set(arrived, mode="drop")
    )
    band_cols = (
        jnp.zeros((band_rows,), jnp.int32)
        .at[arrived_tags[:, 0]]
        .set(arrived_tags[:, 1], mode="drop")
    )
    home_row = (my_row + my_col) % grid_rows
    chosen = jnp.arange(grid_rows, dtype=jnp.int32) == home_row
    window_out = jnp.where(
        chosen[:, None, None, None],
        band_blocks[None, :window_rows],
        jnp.zeros((), owned_blocks.dtype),
    )
    window_tags = jnp.where(chosen[:, None], band_cols[None, :window_rows], 0)
    window_in, window_tags_in = (
        lax.all_to_all(window_out, "row", split_axis=0, concat_axis=0, tiled=True),
        lax.all_to_all(window_tags, "row", split_axis=0, concat_axis=0, tiled=True),
    )
    source_row = (my_row - my_col) % grid_rows
    window_piece = lax.dynamic_index_in_dim(window_in, source_row, 0, keepdims=False)
    window_piece_tags = lax.dynamic_index_in_dim(window_tags_in, source_row, 0, keepdims=False)
    every_blocks, every_tags = (
        lax.all_gather(window_piece, "col", axis=0, tiled=True),
        lax.all_gather(window_piece_tags, "col", axis=0, tiled=True),
    )
    every_blocks = every_blocks.reshape(grid_cols, window_rows, block_size, block_size)
    every_tags = every_tags.reshape(grid_cols, window_rows)
    within = jnp.arange(window_rows, dtype=jnp.int32)
    halves = jnp.arange(2, dtype=jnp.int32)
    square = jnp.zeros((group_cols, window_rows, block_size, block_size), jnp.float32)
    all_cols = lax.all_gather(band_cols, "row", axis=0, tiled=True)
    stored_cols = all_cols.reshape(grid_rows, band_rows)
    current = band_blocks
    kept_list = []
    for section_index in range(grid_rows):
        band_id = (my_row + my_col + section_index) % grid_rows
        source_cols = lax.dynamic_index_in_dim(
            stored_cols, (band_id - my_col) % grid_rows, 0, keepdims=False
        )
        groups = band_id + grid_rows * halves
        left_blocks = every_blocks[groups]
        first_inner_row = halves[:, None] * group_cols + every_tags[groups]
        first_right_blocks = current[first_inner_row]
        first_target = source_cols[first_inner_row]
        first_products = jnp.einsum(
            "uiab,uibc->uiac", left_blocks, first_right_blocks, preferred_element_type=jnp.float32
        )
        square = square.at[first_target, jnp.broadcast_to(within[None, :], first_target.shape)].add(
            first_products
        )
        kept_list.append(current)
        if section_index + 1 < grid_rows:
            current = passed_along(current, "row", -1)
    stored = jnp.stack(kept_list)
    block_base = my_row + my_col
    keep_mask = keep.T.astype(jnp.float32)[:, :, None, None]
    filtered = (square * keep_mask).astype(jnp.bfloat16)
    piece = lax.all_gather(filtered, "col", axis=0, tiled=True)
    piece_rows = piece.shape[0]
    positions = jnp.arange(piece_rows, dtype=jnp.int32)
    kgroup = positions // group_cols
    band_id = kgroup % grid_rows
    inner_row = kgroup // grid_rows * group_cols + positions % group_cols
    right_blocks = stored[(band_id - block_base) % grid_rows, inner_row]
    target = stored_cols[(band_id - my_col) % grid_rows, inner_row]
    products = jnp.einsum("mrab,mbc->mrac", piece, right_blocks, preferred_element_type=jnp.float32)
    cubed = (
        jnp.zeros((group_cols, window_rows, block_size, block_size), jnp.float32)
        .at[target]
        .add(products)
    )
    purified = (3.0 * filtered.astype(jnp.float32) - 2.0 * cubed).astype(jnp.bfloat16)
    return purified.transpose(1, 2, 0, 3).reshape(window_rows * block_size, group_cols * block_size)


def solution(mesh):
    placed = (
        P(("row", "col"), None, None, None),
        P(("row", "col")),
        P(("row", "col"), None),
        P("row", "col"),
    )
    return jax.shard_map(
        local, mesh=mesh, in_specs=placed, out_specs=P("row", "col"), check_vma=False
    )
```

profile of v0, /device:TPU:0, one launch (start us, length us, event | category | flops | bytes accessed | tf_op | source)
XLA Modules:
  0.0 709.8 jit_solution(11088645323843346324)
XLA Ops:
  7.5 2.7 gather_fusion.1
  10.4 2.4 gather_fusion
  13.6 7.3 %all-to-all-start = ((s32[32,8,2]{1,2,0:T(2,128)}), s32[32,8,2]{1,2,0:T(2,128)S(1)}, u32[]{:S(2)}, u32[]{:S(2)}) async-start(s32[32,8,2]{1,2,0:T(2,128)} %copy.23), calls=%async_computation | async-start | bytes 65536 | tf_op jit(solution)/shard_map/all_to_all | solution.py:42
  20.9 14.2 %gather_fusion.4 = bf16[256,128,128]{2,1,0:T(8,128)(2,1)} fusion(bf16[4,8,8,128,128]{4,3,2,1,0:T(8,128)(2,1)} %bitcast.118, s32[256]{0:T(256)S(1)} %reshape.641), kind=kCustom, calls=%fused_computation.4 | custom fusion | bytes 16780288 | tf_op jit(solution)/shard_map/gather | solution.py:30
  35.1 6.0 all-to-all-start.2
  41.2 184.7 %all-to-all-done.2 = bf16[32,8,128,128]{3,2,1,0:T(8,128)(2,1)} async-done(((bf16[32,8,128,128]{3,2,1,0:T(8,128)(2,1)}), bf16[32,8,128,128]{3,2,1,0:T(8,128)(2,1)}, u32[]{:S(2)}, u32[]{:S(2)}) %all-to-all-start.2) | async-done | bytes 8388640 | tf_op jit(solution)/shard_map/all_to_all | solution.py:35
  226.4 23.9 %scatter_fusion = bf16[64,128,128]{2,1,0:T(8,128)(2,1)S(1)} fusion(bf16[64,128,128]{2,1,0:T(8,128)(2,1)S(1)} %broadcast_in_dim.72, s32[256]{0:T(256)S(1)} %bitcast.133, bf16[256,128,128]{2,1,0:T(8,128)(2,1)} %bitcast.10), kind=kCustom, calls=%fused_computation.22 | custom fusion | bytes 25166848 | tf_op jit(solution)/shard_map/scatter | solution.py:55
  251.0 46.7 %collective-permute-done = bf16[64,128,128]{2,1,0:T(8,128)(2,1)} collective-permute-done((bf16[64,128,128]{2,1,0:T(8,128)(2,1)S(1)}, bf16[64,128,128]{2,1,0:T(8,128)(2,1)}, u32[]{:S(2)}, u32[]{:S(2)}) %collective-permute-start) | collective-permute-done | bytes 2097184 | tf_op jit(solution)/shard_map/ppermute | solution.py:9
  304.6 3.2 all-to-all-start.1
  308.1 40.0 %all-reduce = s32[256]{0:T(256)S(1)} all-reduce(s32[256]{0:T(256)S(1)} %dynamic-update-slice), channel_id=1, replica_groups=mesh['row'=4,'col'=8] {'row'}, use_global_device_ids=true, to_apply=%add | all-reduce | flops 256 | bytes 2048
  348.3 6.4 all-reduce.1
  357.1 2.6 collective-permute-start.2
  363.9 3.4 all-to-all-start.3
  368.1 36.6 %all-to-all-done.3 = bf16[4,2,128,128]{3,2,1,0:T(8,128)(2,1)S(1)} async-done(((bf16[4,2,128,128]{3,2,1,0:T(8,128)(2,1)}), bf16[4,2,128,128]{3,2,1,0:T(8,128)(2,1)S(1)}, u32[]{:S(2)}, u32[]{:S(2)}) %all-to-all-start.3) | async-done | bytes 262176 | tf_op jit(solution)/shard_map/all_to_all | solution.py:71
  404.7 16.5 %all-gather.1 = bf16[1,16,128,128]{3,2,0,1:T(8,128)(2,1)S(1)} all-gather(bf16[1,2,128,128]{3,2,0,1:T(8,128)(2,1)S(1)} %dynamic-slice_bitcast_fusion), channel_id=3, replica_groups=mesh['row'=4,'col'=8] {'col'}, dimensions={1}, use_global_device_ids=true | all-gather | bytes 589824 | tf_op jit(solution)/shard_map/all_gather | solution.py:78
  423.7 2.4 broadcast.829.clone
  426.2 2.3 scatter_fusion.1
  428.5 2.2 gather_fusion.10
  430.8 2.3 scatter_fusion.2
  435.5 2.3 scatter_fusion.3
  437.8 2.2 gather_fusion.18
  440.2 2.3 scatter_fusion.4
  442.5 3.9 multiply_convert_fusion
  446.5 2.4 gather_fusion.19
  449.0 6.6 pad_maximum_fusion
  455.6 14.7 %gather_fusion.20 = bf16[256,128,128]{2,1,0:T(8,128)(2,1)} fusion(bf16[4,64,128,128]{3,2,1,0:T(8,128)(2,1)} %pad_maximum_fusion, s32[256]{0:T(256)S(1)} %bitcast.116), kind=kCustom, calls=%fused_computation.20 | custom fusion | bytes 16779264 | tf_op jit(solution)/shard_map/gather | solution.py:119
  470.3 128.6 %all-gather.4.cloned.1.call-done = bf16[256,2,128,128]{3,2,1,0:T(8,128)(2,1)} async-done(((bf16[32,2,128,128]{3,2,1,0:T(8,128)(2,1)}), bf16[256,2,128,128]{3,2,1,0:T(8,128)(2,1)}) %all-gather.4.cloned.1.call-update) | async-done | bytes 16777232 | tf_op jit(solution)/shard_map/all_gather | solution.py:113
  599.0 18.8 %fusion = f32[256,2,128,128]{3,2,1,0:T(8,128)} fusion(bf16[256,2,128,128]{3,2,1,0:T(8,128)(2,1)} %all-gather.4.cloned.1.call-done, bf16[256,128,128]{2,1,0:T(8,128)(2,1)} %gather_fusion.20), kind=kOutput, calls=%fused_computation.29 | convolution fusion | flops 2147483648 | bytes 58720256 | tf_op jit(solution)/shard_map/mrab,mbc->mrac/dot_general | solution.py:121
  617.8 2.6 broadcast.829
  620.4 74.3 %scatter_fusion.5 = f32[32,2,128,128]{3,2,1,0:T(8,128)} fusion(f32[32,2,128,128]{3,2,1,0:T(8,128)} %broadcast.829, s32[256]{0:T(256)S(1)} %bitcast.132, f32[256,2,128,128]{3,2,1,0:T(8,128)} %fusion), kind=kCustom, calls=%fused_computation.27 | custom fusion | flops 8388608 | bytes 100664320 | tf_op jit(solution)/shard_map/scatter-add | solution.py:125
  694.6 4.6 fusion.2
  700.6 2.3 copy.31
  (97 shorter events, 23.1 us)
Async XLA Ops:
  7.5 2.8 copy-start.1
  13.6 21.5 %all-to-all-start = ((s32[32,8,2]{1,2,0:T(2,128)}), s32[32,8,2]{1,2,0:T(2,128)S(1)}, u32[]{:S(2)}, u32[]{:S(2)}) async-start(s32[32,8,2]{1,2,0:T(2,128)} %copy.23), calls=%async_computation | async-start | bytes 65536 | tf_op jit(solution)/shard_map/all_to_all | solution.py:42
  35.1 190.8 %all-to-all-start.2 = ((bf16[32,8,128,128]{3,2,1,0:T(8,128)(2,1)}), bf16[32,8,128,128]{3,2,1,0:T(8,128)(2,1)}, u32[]{:S(2)}, u32[]{:S(2)}) async-start(bf16[32,8,128,128]{3,2,1,0:T(8,128)(2,1)} %bitcast.115), calls=%async_computation.2 | async-start | bytes 16777216 | tf_op jit(solution)/shard_map/all_to_all | solution.py:35
  226.4 73.5 %copy-start.3 = (u32[32]{0:T(128)S(1)}, u32[32]{0:T(128)}, u32[]{:S(2)}) copy-start(u32[32]{0:T(128)} %constant.326) | copy-start | bytes 388
  226.4 74.1 %copy-start.2 = (u32[32]{0:T(128)S(1)}, u32[32]{0:T(128)}, u32[]{:S(2)}) copy-start(u32[32]{0:T(128)} %constant.321) | copy-start | bytes 388
  226.4 74.7 %copy-start = (s32[2,32]{1,0:T(2,128)S(1)}, s32[2,32]{1,0:T(2,128)}, u32[]{:S(2)}) copy-start(s32[2,32]{1,0:T(2,128)} %param.7) | copy-start | bytes 772
  250.3 47.4 %collective-permute-start = (bf16[64,128,128]{2,1,0:T(8,128)(2,1)S(1)}, bf16[64,128,128]{2,1,0:T(8,128)(2,1)}, u32[]{:S(2)}, u32[]{:S(2)}) collective-permute-start(bf16[64,128,128]{2,1,0:T(8,128)(2,1)S(1)} %scatter_fusion), channel_id=1, source_target_pairs={{0,24},{8,0},{16,8},{24,16},{1,25},{9,1},{17,9},{25,17},{2,26},{10... | collective-permute-start | bytes 6291464 | tf_op jit(solution)/shard_map/ppermute | solution.py:9
  297.8 59.4 %collective-permute-start.1 = (bf16[64,128,128]{2,1,0:T(8,128)(2,1)}, bf16[64,128,128]{2,1,0:T(8,128)(2,1)}, u32[]{:S(2)}, u32[]{:S(2)}) collective-permute-start(bf16[64,128,128]{2,1,0:T(8,128)(2,1)} %collective-permute-done), channel_id=1, source_target_pairs={{0,24},{8,0},{16,8},{24,16},{1,25},{9,1},{17,9},{25,17},{2,26},{10... | collective-permute-start | bytes 6291464 | tf_op jit(solution)/shard_map/ppermute | solution.py:9
  304.6 43.6 %all-to-all-start.1 = ((s32[4,1,2]{2,1,0:T(1,128)}), s32[4,1,2]{2,1,0:T(1,128)S(1)}, u32[]{:S(2)}, u32[]{:S(2)}) async-start(s32[4,1,2]{2,1,0:T(1,128)} %broadcast_select_fusion.1), calls=%async_computation.1 | async-start | bytes 4096 | tf_op jit(solution)/shard_map/all_to_all | solution.py:72
  357.1 80.7 %collective-permute-start.2 = (bf16[64,128,128]{2,1,0:T(8,128)(2,1)}, bf16[64,128,128]{2,1,0:T(8,128)(2,1)}, u32[]{:S(2)}, u32[]{:S(2)}) collective-permute-start(bf16[64,128,128]{2,1,0:T(8,128)(2,1)} %collective-permute-done.1), channel_id=1, source_target_pairs={{0,24},{8,0},{16,8},{24,16},{1,25},{9,1},{17,9},{25,17},{2,26},{10... | collective-permute-start | bytes 6291464 | tf_op jit(solution)/shard_map/ppermute | solution.py:9
  363.9 40.8 %all-to-all-start.3 = ((bf16[4,2,128,128]{3,2,1,0:T(8,128)(2,1)}), bf16[4,2,128,128]{3,2,1,0:T(8,128)(2,1)S(1)}, u32[]{:S(2)}, u32[]{:S(2)}) async-start(bf16[4,2,128,128]{3,2,1,0:T(8,128)(2,1)} %broadcast_select_fusion), calls=%async_computation.3 | async-start | bytes 524288 | tf_op jit(solution)/shard_map/all_to_all | solution.py:71
  367.3 231.7 %all-gather.4.cloned.1.call-start = ((), (), s32[]{:S(2)}) async-start(), calls=%async_computation.4 | async-start | bytes 18874368 | tf_op jit(solution)/shard_map/all_gather | solution.py:113
Sparse Core Ops, SparseCore 0:
  446.6 152.3 all-gather.3
where the time goes:
time: 712 us; the launch traced here: 710 us
  waiting for transfers between devices  397 us (56%)
  other arithmetic  101 us (14%)
  local copies, waits for them, and re-layouts  89.8 us (13%)
  blocking collectives  62.9 us (9%)
  starting transfers between devices  25.4 us (4%)
  matrix products  19.5 us (3%)
  between operations  15 us (2%)
    all_to_all x1, waiting for transfers between devices, local(): lax.all_to_all(outgoing.reshape(grid_rows * grid_cols, per_band, block_si...  185 us
    all_gather x1, waiting for transfers between devices, local(): piece = lax.all_gather(filtered, 'col', axis=0, tiled=True)  129 us
    scatter-add x1, other arithmetic, local(): cubed = jnp.zeros((group_cols, window_rows, block_size, block_size), jnp....  74.3 us
    ppermute x3, waiting for transfers between devices, passed_along(): lax.ppermute(value, axis, [(i, (i + by) % devices) for i in range(devices)])  46.7 us
    unnamed x2, blocking collectives  46.4 us
    all_to_all x1, waiting for transfers between devices, local(): lax.all_to_all(window_out, 'row', split_axis=0, concat_axis=0, tiled=True)  36.6 us
    scatter x1, local copies, waits for them, and re-layouts, local(): band_blocks = jnp.zeros((band_rows, block_size, block_size), owned_blocks...  23.9 us
    dot_general x1, matrix products, local(): jnp.einsum('mrab,mbc->mrac', piece, right_blocks, preferred_element_type=...  18.8 us
  transfers between devices with their start and end apart: 8, of which 4 were waited for; matrix products, arithmetic and copies ran while one was open for 9% of the time, Pallas kernels for 0%

commit v1 on v0

v1 whole, which is shorter than its diff:
```python
import functools

import jax
import jax.numpy as jnp
from jax import lax
from jax.experimental import pallas as pl
from jax.experimental.pallas import tpu as pltpu
from jax.sharding import PartitionSpec as P

MESH = pl.DeviceIdType.MESH
ANY = pl.BlockSpec(memory_space=pl.ANY)
SMEM = pl.BlockSpec(memory_space=pltpu.SMEM)
VMEM = pl.BlockSpec(memory_space=pltpu.VMEM)
DMA = pltpu.SemaphoreType.DMA
BIG = 60 * 1024 * 1024


def remote_params(number):
    return pltpu.CompilerParams(collective_id=number, has_side_effects=True)


def spread_kernel(n_row, n_col, meta, owned, meta_all, sibling, send, recv, pair_send, pair_recv):
    r, c = lax.axis_index("row"), lax.axis_index("col")
    me = r * n_col + c
    devices = n_row * n_col
    barrier = pltpu.get_barrier_semaphore()

    def greet(i, carry):
        d = lax.rem(me + i, devices)
        pl.semaphore_signal(barrier, inc=1, device_id=(d // n_col, lax.rem(d, n_col)), device_id_type=MESH)
        return carry

    lax.fori_loop(1, devices, greet, 0)
    pl.semaphore_wait(barrier, devices - 1)
    z, k = c // 2, lax.rem(c, 2)
    other = 1 - k
    pair = pltpu.make_async_remote_copy(
        src_ref=owned.at[:, :, other], dst_ref=sibling, send_sem=pair_send, recv_sem=pair_recv,
        device_id=(r, 2 * z + other), device_id_type=MESH)
    pair.start()

    def copy_to(i):
        d = lax.rem(me + i, devices)
        return pltpu.make_async_remote_copy(
            src_ref=meta, dst_ref=meta_all.at[me], send_sem=send.at[i], recv_sem=recv.at[i],
            device_id=(d // n_col, lax.rem(d, n_col)), device_id_type=MESH)

    def begin(i, carry):
        copy_to(i).start()
        return carry

    def finish(i, carry):
        copy_to(i).wait()
        return carry

    lax.fori_loop(1, devices, begin, 0)
    lax.fori_loop(1, devices, finish, 0)
    pair.wait()


def along_z_kernel(nz, source, got, send, recv):
    r, c = lax.axis_index("row"), lax.axis_index("col")
    z, k = c // 2, lax.rem(c, 2)
    barrier = pltpu.get_barrier_semaphore()
    for step in range(1, nz):
        to = lax.rem(z + step, nz)
        pl.semaphore_signal(barrier, inc=1, device_id=(r, 2 * to + k), device_id_type=MESH)
    pl.semaphore_wait(barrier, nz - 1)
    copies = []
    for step in range(1, nz):
        to = lax.rem(z + step, nz)
        copies.append(pltpu.make_async_remote_copy(
            src_ref=source.at[to], dst_ref=got.at[z], send_sem=send.at[step], recv_sem=recv.at[step],
            device_id=(r, 2 * to + k), device_id_type=MESH))
    for copy in copies:
        copy.start()
    for copy in copies:
        copy.wait()


def in_plane_kernel(n_row, source, got, send, recv):
    r, c = lax.axis_index("row"), lax.axis_index("col")
    barrier = pltpu.get_barrier_semaphore()
    for step in range(1, n_row):
        pl.semaphore_signal(barrier, inc=1, device_id=(lax.rem(r + step, n_row), c), device_id_type=MESH)
    pl.semaphore_wait(barrier, n_row - 1)
    copies = []
    for step in range(1, n_row):
        to = lax.rem(r + step, n_row)
        copies.append(pltpu.make_async_remote_copy(
            src_ref=source.at[to], dst_ref=got.at[r], send_sem=send.at[step], recv_sem=recv.at[step],
            device_id=(to, c), device_id_type=MESH))
    for copy in copies:
        copy.start()
    for copy in copies:
        copy.wait()


def left_kernel(n_col, piece, got, send, recv):
    r, c = lax.axis_index("row"), lax.axis_index("col")
    barrier = pltpu.get_barrier_semaphore()
    for step in range(1, n_col):
        pl.semaphore_signal(barrier, inc=1, device_id=(r, lax.rem(c + step, n_col)), device_id_type=MESH)
    pl.semaphore_wait(barrier, n_col - 1)
    copies = []
    for step in range(1, n_col):
        copies.append(pltpu.make_async_remote_copy(
            src_ref=piece, dst_ref=got.at[c], send_sem=send.at[step], recv_sem=recv.at[step],
            device_id=(r, lax.rem(c + step, n_col)), device_id_type=MESH))
    for copy in copies:
        copy.start()
    for copy in copies:
        copy.wait()


def last_kernel(n_row, nz, source, filtered, got, every, send, recv, fsend, frecv, psend, precv):
    r, c = lax.axis_index("row"), lax.axis_index("col")
    z, k = c // 2, lax.rem(c, 2)
    mate = (r, 2 * z + 1 - k)
    barrier = pltpu.get_barrier_semaphore()
    for step in range(1, n_row):
        pl.semaphore_signal(barrier, inc=1, device_id=(lax.rem(r + step, n_row), c), device_id_type=MESH)
    for step in range(1, nz):
        pl.semaphore_signal(barrier, inc=1, device_id=(r, 2 * lax.rem(z + step, nz) + k), device_id_type=MESH)
    pl.semaphore_signal(barrier, inc=1, device_id=mate, device_id_type=MESH)
    pl.semaphore_wait(barrier, n_row + nz - 1)
    copies = []
    for step in range(1, nz):
        copies.append(pltpu.make_async_remote_copy(
            src_ref=filtered, dst_ref=every.at[c], send_sem=fsend.at[step], recv_sem=frecv.at[step],
            device_id=(r, 2 * lax.rem(z + step, nz) + k), device_id_type=MESH))
    plane = []
    for step in range(1, n_row):
        to = lax.rem(r + step, n_row)
        plane.append(pltpu.make_async_remote_copy(
            src_ref=source.at[to], dst_ref=got.at[r], send_sem=send.at[step], recv_sem=recv.at[step],
            device_id=(to, c), device_id_type=MESH))
    for copy in copies + plane:
        copy.start()
    pairs = [pltpu.make_async_remote_copy(
        src_ref=filtered, dst_ref=every.at[c], send_sem=psend.at[0], recv_sem=precv.at[0],
        device_id=mate, device_id_type=MESH)]
    pairs[0].start()
    for step in range(1, nz):
        copies[step - 1].wait_recv()
        origin = 2 * lax.rem(z - step + nz, nz) + k
        pair = pltpu.make_async_remote_copy(
            src_ref=every.at[origin], dst_ref=every.at[origin], send_sem=psend.at[step], recv_sem=precv.at[step],
            device_id=mate, device_id_type=MESH)
        pair.start()
        pairs.append(pair)
    for copy in copies:
        copy.wait_send()
    for pair in pairs:
        pair.wait()
    for copy in plane:
        copy.wait()


def pick(first, second, index, dest, sem):
    limit = first.shape[0]

    @pl.when(index < limit)
    def _():
        pltpu.make_async_copy(first.at[index], dest, sem).start()

    @pl.when(index >= limit)
    def _():
        pltpu.make_async_copy(second.at[index - limit], dest, sem).start()


def gather_kernel(index, first, second, out, sem):
    start = pl.program_id(0) * out.shape[0]

    def begin(i, carry):
        pick(first, second, index[start + i], out.at[i], sem)
        return carry

    lax.fori_loop(0, out.shape[0], begin, 0)
    pltpu.make_async_copy(out, out, sem).wait()


def gather(index, first, second):
    block = first.shape[-2:]
    count = index.shape[0]
    chunk = max(n for n in range(1, min(count, 512) + 1) if count % n == 0)
    return pl.pallas_call(
        gather_kernel,
        grid=(count // chunk,),
        out_shape=jax.ShapeDtypeStruct((count,) + block, first.dtype),
        in_specs=[SMEM, ANY, ANY], out_specs=pl.BlockSpec((chunk,) + block, lambda i: (i, 0, 0)),
        scratch_shapes=[DMA],
        compiler_params=pltpu.CompilerParams(vmem_limit_bytes=BIG),
    )(index, first.reshape((-1,) + block), second.reshape((-1,) + block))


def square_kernel(left_at, right_at, slot, keep, lefts, own_left, rights, own_rights, out, a, b, acc, sems):
    count = out.shape[0]

    def begin(i, carry):
        pick(lefts, own_left, left_at[i], a.at[i], sems.at[0])
        pick(rights, own_rights, right_at[i], b.at[i], sems.at[1])
        return carry

    lax.fori_loop(0, count, begin, 0)
    acc[...] = jnp.zeros_like(acc)
    pltpu.make_async_copy(a, a, sems.at[0]).wait()
    pltpu.make_async_copy(b, b, sems.at[1]).wait()

    def multiply(i, carry):
        acc[slot[i]] += jnp.dot(a[i], b[i], preferred_element_type=jnp.float32)
        return carry

    lax.fori_loop(0, count, multiply, 0)

    def write(i, carry):
        out[i] = (acc[i] * keep[i].astype(jnp.float32)).astype(out.dtype)
        return carry

    lax.fori_loop(0, count, write, 0)


def cubed_kernel(left_at, right_at, target, own_target, every, own, rights, own_rights, out, a, b, f, acc, sems):
    count = a.shape[0]
    windows = acc.shape[0]
    block = a.shape[-1]
    per_window = count // windows
    own_per_window = f.shape[0] // windows

    def begin(i, carry):
        pick(every, own, left_at[i], a.at[i], sems.at[0])
        pick(rights, own_rights, right_at[i], b.at[i], sems.at[1])
        return carry

    lax.fori_loop(0, count, begin, 0)
    mine = pltpu.make_async_copy(own, f, sems.at[2])
    mine.start()
    acc[...] = jnp.zeros_like(acc)
    pltpu.make_async_copy(a, a, sems.at[0]).wait()
    pltpu.make_async_copy(b, b, sems.at[1]).wait()
    mine.wait()
    for w in range(windows):
        def multiply(i, carry):
            e = w * per_window + i
            acc[w, target[e]] += jnp.dot(a[e], b[e], preferred_element_type=jnp.float32)
            return carry

        lax.fori_loop(0, per_window, multiply, 0)
    acc[...] = -2.0 * acc[...]
    for w in range(windows):
        def add(i, carry):
            e = w * own_per_window + i
            acc[w, own_target[e]] += 3.0 * f[e].astype(jnp.float32)
            return carry

        lax.fori_loop(0, own_per_window, add, 0)
    for w in range(windows):
        for j in range(acc.shape[1]):
            out[w * block:(w + 1) * block, j * block:(j + 1) * block] = acc[w, j].astype(out.dtype)


def running(mask):
    n = mask.shape[-1]
    before = (jnp.arange(n)[:, None] < jnp.arange(n)[None, :]).astype(jnp.bfloat16)
    flat = mask.reshape(-1, n).astype(jnp.bfloat16)
    return jnp.dot(flat, before, preferred_element_type=jnp.float32).astype(jnp.int32).reshape(mask.shape)


def local(owned_blocks, owned_rows, owned_cols, keep):
    n_row, n_col = lax.axis_size("row"), lax.axis_size("col")
    devices = n_row * n_col
    nz = n_col // 2
    r, c = lax.axis_index("row"), lax.axis_index("col")
    z, k = c // 2, lax.rem(c, 2)
    block = owned_blocks.shape[-1]
    dtype = owned_blocks.dtype
    slots = owned_rows.shape[0]
    per_band = slots // n_row
    windows, gcols = keep.shape
    nb = gcols * n_col
    size = slots * (1 + n_col)
    tall = -(-size // 1024) * 8
    one = (block, block)

    packed = jnp.concatenate([owned_rows[:, None], owned_cols], axis=1).reshape(-1)
    meta = jnp.pad(packed, (0, tall * 128 - size)).reshape(tall, 128)
    meta_all, sibling = pl.pallas_call(
        functools.partial(spread_kernel, n_row, n_col),
        out_shape=(jax.ShapeDtypeStruct((devices, tall, 128), jnp.int32),
                   jax.ShapeDtypeStruct((slots, nz) + one, dtype)),
        in_specs=[ANY, ANY], out_specs=(ANY, ANY),
        scratch_shapes=[DMA((devices,)), DMA((devices,)), DMA, DMA],
        compiler_params=remote_params(0),
    )(meta, owned_blocks.reshape((slots, nz, 2) + one))
    me = r * n_col + c
    is_me = jnp.arange(devices)[:, None] == me
    labels = jnp.where(is_me, packed[None, :], meta_all.reshape(devices, -1)[:, :size])
    labels = labels.reshape(devices * slots, 1 + n_col)
    rows, cols = labels[:, 0], labels[:, 1:]
    filled = rows < gcols * 2
    band = jnp.arange(devices * slots, dtype=jnp.int32) // per_band % n_row
    row_id = jnp.where(filled, gcols * (band + n_row * (rows // gcols)) + rows % gcols, nb)
    chips = devices // 2
    pool = 2 * slots
    filled_pool = filled.reshape(chips, pool)
    place = running(filled_pool)
    chip_count = filled_pool.sum(axis=1)
    hit = row_id[None, :] == jnp.arange(nb, dtype=jnp.int32)[:, None]

    def at_row(values):
        return jnp.sum(jnp.where(hit, values[None, :], 0), axis=1)

    chip = at_row(jnp.arange(devices * slots, dtype=jnp.int32) // pool)
    spot = at_row(place.reshape(-1))
    row_cols = jnp.sum(jnp.where(hit[:, :, None], cols[None, :, :], 0), axis=1)
    line, plane = chip // nz, chip % nz

    base = gcols * jnp.arange(n_col, dtype=jnp.int32)
    window = gcols * jnp.arange(n_row, dtype=jnp.int32)[:, None] + jnp.arange(windows, dtype=jnp.int32)[None, :]
    inner = base + row_cols[window]
    targets = base + row_cols[inner]
    every_row = jnp.arange(nb, dtype=jnp.int32)
    need1 = jnp.any(inner.reshape(n_row, -1, 1) == every_row, axis=1)
    need1 = need1 | jnp.any(window[:, :, None] == every_row, axis=1)
    need2 = jnp.any(targets.reshape(n_row, -1, 1) == every_row, axis=1)
    on_line = line[None, :] == jnp.arange(n_row, dtype=jnp.int32)[:, None]

    def ranks(need):
        both = need[:, None, :] & on_line[None, :, :]
        rank = jnp.sum(jnp.where(both, running(both), 0), axis=1)
        return rank, both.sum(axis=2).max()

    rank1, most1 = ranks(need1)
    rank2, most2 = ranks(need2)
    fits_chip = chip_count.max()

    inner_mine = inner[r].reshape(-1)
    targets_mine = targets[r].reshape(-1)
    cols_mine = lax.dynamic_index_in_dim(row_cols, c, 1, keepdims=False)
    square_target = cols_mine[inner_mine].reshape(windows, n_col)
    same = square_target[:, :, None] == square_target[:, None, :]
    first = jnp.argmax(same, axis=2).astype(jnp.int32)
    square_slot = (first + n_col * jnp.arange(windows, dtype=jnp.int32)[:, None]).reshape(-1)
    kept = jnp.take_along_axis(keep, square_target, axis=1).reshape(-1)
    cubed_target = cols_mine[targets_mine]
    entries = windows * n_col

    def run(caps, number):
        cap, cap1, cap2 = caps
        mine = lax.dynamic_index_in_dim(jnp.where(filled_pool, place, pool), r * nz + z, 0, keepdims=False)
        pick_slot = jnp.sum(
            jnp.where(mine[None, :] == jnp.arange(cap)[:, None], jnp.arange(pool, dtype=jnp.int32)[None, :], 0), axis=1)
        zs = jnp.arange(nz, dtype=jnp.int32)[:, None]
        at = pick_slot[None, :] % slots
        index = jnp.where(
            pick_slot[None, :] // slots == k, at * n_col + 2 * zs + k, slots * n_col + at * nz + zs)
        outgoing = gather(index.reshape(-1), owned_blocks, sibling).reshape((nz, cap) + one)
        got = pl.pallas_call(
            functools.partial(along_z_kernel, nz),
            out_shape=jax.ShapeDtypeStruct((nz, cap) + one, dtype),
            in_specs=[ANY], out_specs=ANY,
            scratch_shapes=[DMA((nz,)), DMA((nz,))],
            compiler_params=remote_params(number),
        )(outgoing)
        held_at = plane * cap + spot + jnp.where(plane == z, nz * cap, 0)

        def demand(need, rank, limit):
            sending = need & (line == r)[None, :]
            chosen = sending[:, None, :] & (rank[:, None, :] == jnp.arange(limit, dtype=jnp.int32)[None, :, None])
            where = jnp.sum(jnp.where(chosen, held_at[None, None, :], 0), axis=2)
            return gather(where.reshape(-1), got, outgoing).reshape((n_row, limit) + one)

        def found(rank, limit):
            return line * limit + rank[r] + jnp.where(line == r, n_row * limit, 0)

        send1 = demand(need1, rank1, cap1)
        got1 = pl.pallas_call(
            functools.partial(in_plane_kernel, n_row),
            out_shape=jax.ShapeDtypeStruct((n_row, cap1) + one, dtype),
            in_specs=[ANY], out_specs=ANY,
            scratch_shapes=[DMA((n_row,)), DMA((n_row,))],
            compiler_params=remote_params(number + 1),
        )(send1)
        found1 = found(rank1, cap1)
        window_mine = gcols * r + jnp.arange(windows, dtype=jnp.int32)
        left_mine = gather(found1[window_mine], got1, send1)
        lefts = pl.pallas_call(
            functools.partial(left_kernel, n_col),
            out_shape=jax.ShapeDtypeStruct((n_col, windows) + one, dtype),
            in_specs=[ANY], out_specs=ANY,
            scratch_shapes=[DMA((n_col,)), DMA((n_col,))],
            compiler_params=remote_params(number + 2),
        )(left_mine)
        ws = jnp.arange(windows, dtype=jnp.int32)[:, None]
        gs = jnp.arange(n_col, dtype=jnp.int32)[None, :]
        left_at = jnp.where(gs == c, n_col * windows + ws, gs * windows + ws).reshape(-1)
        filtered = pl.pallas_call(
            square_kernel,
            out_shape=jax.ShapeDtypeStruct((entries,) + one, dtype),
            in_specs=[SMEM] * 4 + [ANY] * 4, out_specs=VMEM,
            scratch_shapes=[pltpu.VMEM((entries,) + one, dtype), pltpu.VMEM((entries,) + one, dtype),
                            pltpu.VMEM((entries,) + one, jnp.float32), DMA((2,))],
            compiler_params=pltpu.CompilerParams(vmem_limit_bytes=BIG),
        )(left_at, found1[inner_mine], square_slot, kept, lefts.reshape((-1,) + one), left_mine,
          got1.reshape((-1,) + one), send1.reshape((-1,) + one))
        send2 = demand(need2, rank2, cap2)
        got2, every = pl.pallas_call(
            functools.partial(last_kernel, n_row, nz),
            out_shape=(jax.ShapeDtypeStruct((n_row, cap2) + one, dtype),
                       jax.ShapeDtypeStruct((n_col, entries) + one, dtype)),
            in_specs=[ANY, ANY], out_specs=(ANY, ANY),
            scratch_shapes=[DMA((n_row,)), DMA((n_row,)), DMA((nz,)), DMA((nz,)), DMA((nz,)), DMA((nz,))],
            compiler_params=remote_params(number + 3),
        )(send2, filtered)
        found2 = found(rank2, cap2)
        place3 = ws[:, :, None] * n_col + gs[:, :, None]
        groups = jnp.arange(n_col, dtype=jnp.int32)[None, None, :]
        left_at = jnp.where(groups == c, n_col * entries + place3, groups * entries + place3).reshape(-1)
        count = windows * n_col * n_col
        return pl.pallas_call(
            cubed_kernel,
            out_shape=jax.ShapeDtypeStruct((windows * block, gcols * block), dtype),
            in_specs=[SMEM] * 4 + [ANY] * 4, out_specs=VMEM,
            scratch_shapes=[pltpu.VMEM((count,) + one, dtype), pltpu.VMEM((count,) + one, dtype),
                            pltpu.VMEM((entries,) + one, dtype),
                            pltpu.VMEM((windows, gcols) + one, jnp.float32), DMA((3,))],
            compiler_params=pltpu.CompilerParams(vmem_limit_bytes=BIG),
        )(left_at, found2[targets_mine], cubed_target, square_target.reshape(-1), every.reshape((-1,) + one), filtered,
          got2.reshape((-1,) + one), send2.reshape((-1,) + one))

    most_demand = windows * n_col * n_col
    full = (pool, windows * (n_col + 1), min(most_demand, nb, n_col * slots))
    small = (pool // 2, windows * (n_col + 1) * 2 // 3, 5 * most_demand // (4 * n_row) if n_row == 4 else most_demand // 4)
    fits = (fits_chip <= small[0]) & (most1 <= small[1]) & (most2 <= small[2])
    return lax.cond(fits, lambda: run(small, 1), lambda: run(full, 5))


def solution(mesh):
    placed = (
        P(("row", "col"), None, None, None),
        P(("row", "col")),
        P(("row", "col"), None),
        P("row", "col"),
    )
    return jax.shard_map(
        local, mesh=mesh, in_specs=placed, out_specs=P("row", "col"), check_vma=False
    )
```

time: 712 us -> 285 us (0.40)
  waiting for transfers between devices: 397 us -> 0 us
  Pallas kernels: 0 us -> 251 us
  other arithmetic: 101 us -> 11.1 us
  local copies, waits for them, and re-layouts: 89.8 us -> 17.8 us
  blocking collectives: 62.9 us -> 0 us
  starting transfers between devices: 25.4 us -> 0 us
  matrix products: 19.5 us -> 0.43 us
  between operations: 15 us -> 2.17 us
    pallas_call x0 -> x11, Pallas kernels: none -> 251 us  [the longest x1 72.3 us: run(): pl.pallas_call(functools.partial(along_z_kernel, nz), out_shape=jax.Shape...]
    all_to_all x4 -> x0, waiting for transfers between devices: 221 us -> none  [the longest x1 185 us: local(): lax.all_to_all(outgoing.reshape(grid_rows * grid_cols, per_band, block_si...]
    all_gather x1 -> x0, waiting for transfers between devices: 129 us -> none  [local(): piece = lax.all_gather(filtered, 'col', axis=0, tiled=True)]
    scatter-add x5 -> x0, other arithmetic: 83.6 us -> none  [the longest x1 74.3 us: local(): cubed = jnp.zeros((group_cols, window_rows, block_size, block_size), jnp....]
    ppermute x3 -> x0, waiting for transfers between devices: 46.7 us -> none  [passed_along(): lax.ppermute(value, axis, [(i, (i + by) % devices) for i in range(devices)])]
    unnamed x2 -> x0, blocking collectives: 46.4 us -> none
    gather x25 -> x10, local copies, waits for them, and re-layouts: 50.9 us -> 8.5 us  [the longest x1 1.79 us: run(): found2[targets_mine]]
    scatter x2 -> x0, local copies, waits for them, and re-layouts: 25.3 us -> none  [the longest x1 23.9 us: local(): band_blocks = jnp.zeros((band_rows, block_size, block_size), owned_blocks...]
  transfers between devices with their start and end apart: 8 -> 0, of which waited for: 4 -> 0; matrix products, arithmetic and copies ran while one was open for 9% -> 0% of each run, Pallas kernels for 0% -> 0%
where the time goes in v1:
time: 285 us; the launch traced here: 283 us
  Pallas kernels  251 us (88%)
  local copies, waits for them, and re-layouts  17.8 us (6%)
  other arithmetic  11.1 us (4%)
    pallas_call x1, Pallas kernels, run(): pl.pallas_call(functools.partial(along_z_kernel, nz), out_shape=jax.Shape...  72.3 us
    pallas_call x1, Pallas kernels, run(): pl.pallas_call(functools.partial(last_kernel, n_row, nz), out_shape=(jax....  64.5 us
    pallas_call x1, Pallas kernels, run(): pl.pallas_call(functools.partial(left_kernel, n_col), out_shape=jax.Shape...  33.8 us
    pallas_call x1, Pallas kernels, run(): pl.pallas_call(cubed_kernel, out_shape=jax.ShapeDtypeStruct((windows * bl...  23 us
    pallas_call x4, Pallas kernels, gather(): pl.pallas_call(gather_kernel, grid=(count // chunk,), out_shape=jax.Shape...  19.1 us
    pallas_call x1, Pallas kernels, run(): pl.pallas_call(functools.partial(in_plane_kernel, n_row), out_shape=jax.S...  18.5 us
    pallas_call x1, Pallas kernels, local(): pl.pallas_call(functools.partial(spread_kernel, n_row, n_col), out_shape=...  14.9 us

profile of v1, /device:TPU:0, one launch (start us, length us, event | category | flops | bytes accessed | tf_op | source)
XLA Modules:
  0.0 283.1 jit_solution(17660363049950850981)
XLA Ops:
  0.5 0.7 pad_add_fusion
  1.4 0.6 pad_bitcast_fusion.meta
  2.0 14.9 %shard_map.54 = (s32[32,8,128]{2,1,0:T(8,128)}, bf16[32,4,128,128]{3,2,1,0:T(8,128)(2,1)}) custom-call(s32[8,128]{1,0:T(8,128)} %pad_bitcast_fusion.meta, bf16[32,4,2,128,128]{4,3,2,1,0:T(8,128)(2,1)} %bitcast.69), custom_call_target="tpu_custom_call" | custom-call | tf_op jit(solution)/shard_map/pallas_call | solution.py:287
  16.9 0.9 copy.22
  18.9 0.6 reduce_max.27
  21.3 4.4 %select_reduce_fusion.12 = s32[256,8]{1,0:T(8,128)S(1)} fusion(s32[1024,8]{0,1:T(8,128)S(1)} %copy.19, pred[256,1024]{1,0:T(8,128)(4,1)S(1)} %iota_compare_fusion.8), kind=kLoop, calls=%fused_computation.131 | loop fusion | flops 4192256 | bytes 303104 | tf_op jit(solution)/shard_map/reduce_sum | solution.py:315
  26.7 0.7 gather_fusion.12
  27.6 0.7 iota_reduce_fusion
  28.4 0.6 gather_fusion.11
  29.6 0.6 reduce_max.28
  30.9 0.6 reduce_max.29
  32.7 249.1 %conditional.1 = (bf16[256,4096]{1,0:T(8,128)(2,1)S(1)}) conditional(s32[]{:T(128)} %convert_element_type.34, (s32[]{:T(128)}, s32[256]{0:T(256)S(1)}, s32[]{:T(128)}, pred[4,4,256]{2,1,0:T(4,128)(4,1)S(1)}, s32[1,2,8,8]{3,2,1,0:T(8,128)S(1)}, /*index=5*/pred[4,256]{1,0:T(4,128)(4,1)S(1)}, s32[256]{0:T(256)S(1)}, ...), branch_computations={%region_15.19_spmd.clone, %region_19.23_spmd.clone} | conditional | flops 1163009 | bytes 1526950 | solution.py:435
  33.3 0.6 reshape.910.slot
  34.7 0.7 gather_fusion.9
  36.6 5.9 %branch_1_fun.10.second = bf16[128,128,128]{2,1,0:T(8,128)(2,1)} custom-call(s32[128]{0:T(128)} %select_n.433.index, bf16[256,128,128]{2,1,0:T(8,128)(2,1)} %bitcast.71, bf16[128,128,128]{2,1,0:T(8,128)(2,1)} %bitcast.84), custom_call_target="tpu_custom_call" | custom-call | tf_op jit(solution)/shard_map/cond/branch_1_fun/pallas_call | solution.py:187
  42.7 1.8 gather_fusion.8
  44.8 0.6 select_n.421.left_at
  45.7 0.6 reshape.898.index
  46.3 1.1 gather_fusion.7
  47.5 1.1 gather_fusion.6
  48.6 1.8 gather_fusion.5
  50.8 0.6 reshape.904.index
  51.4 72.3 %branch_1_fun.11 = bf16[4,32,128,128]{3,2,1,0:T(8,128)(2,1)} custom-call(bf16[4,32,128,128]{3,2,1,0:T(8,128)(2,1)} %bitcast.74), custom_call_target="tpu_custom_call" | custom-call | tf_op jit(solution)/shard_map/cond/branch_1_fun/pallas_call | solution.py:358
  123.7 3.8 %branch_1_fun.13.second.own_rights = bf16[48,128,128]{2,1,0:T(8,128)(2,1)} custom-call(s32[48]{0:T(128)} %reshape.904.index, bf16[128,128,128]{2,1,0:T(8,128)(2,1)} %bitcast.76, bf16[128,128,128]{2,1,0:T(8,128)(2,1)} %branch_1_fun.10.second), custom_call_target="tpu_custom_call" | custom-call | tf_op jit(solution)/shard_map/cond/branch_1_fun/pallas_call | solution.py:187
  127.6 7.3 %branch_1_fun.12.own_rights = bf16[160,128,128]{2,1,0:T(8,128)(2,1)} custom-call(s32[160]{0:T(256)} %reshape.898.index, bf16[128,128,128]{2,1,0:T(8,128)(2,1)} %bitcast.77, bf16[128,128,128]{2,1,0:T(8,128)(2,1)} %branch_1_fun.10.second), custom_call_target="tpu_custom_call" | custom-call | tf_op jit(solution)/shard_map/cond/branch_1_fun/pallas_call | solution.py:187
  134.9 18.5 %branch_1_fun.14 = bf16[4,12,128,128]{3,2,1,0:T(8,128)(2,1)} custom-call(bf16[4,12,128,128]{3,2,1,0:T(8,128)(2,1)} %bitcast.79), custom_call_target="tpu_custom_call" | custom-call | tf_op jit(solution)/shard_map/cond/branch_1_fun/pallas_call | solution.py:377
  153.3 2.1 branch_1_fun.15.piece.own_left
  155.4 33.8 %branch_1_fun.16 = bf16[8,2,128,128]{3,2,1,0:T(8,128)(2,1)} custom-call(bf16[2,128,128]{2,1,0:T(8,128)(2,1)} %branch_1_fun.15.piece.own_left), custom_call_target="tpu_custom_call" | custom-call | tf_op jit(solution)/shard_map/cond/branch_1_fun/pallas_call | solution.py:387
  189.2 5.1 %branch_1_fun.17.filtered.own = bf16[16,128,128]{2,1,0:T(8,128)(2,1)} custom-call(s32[16]{0:T(128)} %select_n.435.left_at, s32[16]{0:T(128)} %gather_fusion.6, s32[16]{0:T(128)} %reshape.910.slot, s32[16]{0:T(128)} %fusion.11.keep, bf16[16,128,128]{2,1,0:T(8,128)(2,1)} %bitcast.91, bf16[2,128,128]{2,1,0:T(8,128)(2,1)} %branch_1_fun.15.piece.own_left, ...), custom_call_target="tpu_custom_call" | custom-call | tf_op jit(solution)/shard_map/cond/branch_1_fun/pallas_call | solution.py:397
  194.3 64.5 %branch_1_fun.18 = (bf16[4,40,128,128]{3,2,1,0:T(8,128)(2,1)}, bf16[8,16,128,128]{3,2,1,0:T(8,128)(2,1)}) custom-call(bf16[4,40,128,128]{3,2,1,0:T(8,128)(2,1)} %bitcast.75, bf16[16,128,128]{2,1,0:T(8,128)(2,1)} %branch_1_fun.17.filtered.own), custom_call_target="tpu_custom_call" | custom-call | tf_op jit(solution)/shard_map/cond/branch_1_fun/pallas_call | solution.py:407
  258.8 23.0 %branch_1_fun.19 = bf16[256,4096]{1,0:T(8,128)(2,1)S(1)} custom-call(s32[128]{0:T(128)} %select_n.421.left_at, s32[128]{0:T(128)} %gather_fusion.5, s32[128]{0:T(128)} %gather_fusion.8, s32[16]{0:T(128)S(1)} %get-tuple-element.408.own_target, bf16[128,128,128]{2,1,0:T(8,128)(2,1)} %bitcast.89, bf16[16,128,128]{2,1,0:T(8,128)(2,1)} %branch_1_fun.17.filtered.own, ...), custom_call_target="tpu_custom_call" | custom-call | tf_op jit(solution)/shard_map/cond/branch_1_fun/pallas_call | solution.py:420
  281.8 1.3 copy-done.1
  (109 shorter events, 8.6 us)
Async XLA Ops:
  16.9 15.8 %copy-start = (s32[2,32]{1,0:T(2,128)S(1)}, s32[2,32]{1,0:T(2,128)}, u32[]{:S(2)}) copy-start(s32[2,32]{1,0:T(2,128)} %param.9) | copy-start | bytes 772
  281.8 1.3 copy-start.1

commit v2 on v1

v2 whole, which is shorter than its diff:
```python
import functools

import jax
import jax.numpy as jnp
from jax import lax
from jax.experimental import pallas as pl
from jax.experimental.pallas import tpu as pltpu
from jax.sharding import PartitionSpec as P

MESH = pl.DeviceIdType.MESH
ANY = pl.BlockSpec(memory_space=pl.ANY)
SMEM = pl.BlockSpec(memory_space=pltpu.SMEM)
VMEM = pl.BlockSpec(memory_space=pltpu.VMEM)
DMA = pltpu.SemaphoreType.DMA
BIG = 60 * 1024 * 1024


def remote_params(number):
    return pltpu.CompilerParams(collective_id=number, has_side_effects=True)


def spread_kernel(n_row, n_col, meta, owned, meta_all, sibling, send, recv, pair_send, pair_recv):
    r, c = lax.axis_index("row"), lax.axis_index("col")
    me = r * n_col + c
    devices = n_row * n_col
    barrier = pltpu.get_barrier_semaphore()

    def greet(i, carry):
        d = lax.rem(me + i, devices)
        pl.semaphore_signal(barrier, inc=1, device_id=(d // n_col, lax.rem(d, n_col)), device_id_type=MESH)
        return carry

    lax.fori_loop(1, devices, greet, 0)
    pl.semaphore_wait(barrier, devices - 1)
    z, k = c // 2, lax.rem(c, 2)
    other = 1 - k
    pair = pltpu.make_async_remote_copy(
        src_ref=owned.at[:, :, other], dst_ref=sibling, send_sem=pair_send, recv_sem=pair_recv,
        device_id=(r, 2 * z + other), device_id_type=MESH)
    pair.start()

    def copy_to(i):
        d = lax.rem(me + i, devices)
        return pltpu.make_async_remote_copy(
            src_ref=meta, dst_ref=meta_all.at[me], send_sem=send.at[i], recv_sem=recv.at[i],
            device_id=(d // n_col, lax.rem(d, n_col)), device_id_type=MESH)

    def begin(i, carry):
        copy_to(i).start()
        return carry

    def finish(i, carry):
        copy_to(i).wait()
        return carry

    lax.fori_loop(1, devices, begin, 0)
    lax.fori_loop(1, devices, finish, 0)
    pair.wait()


def greet(partners):
    barrier = pltpu.get_barrier_semaphore()
    for partner in partners:
        pl.semaphore_signal(barrier, inc=1, device_id=partner, device_id_type=MESH)
    pl.semaphore_wait(barrier, len(partners))


def send_to(source, dest, sems, step, partner):
    return pltpu.make_async_remote_copy(
        src_ref=source, dst_ref=dest, send_sem=sems[0].at[step], recv_sem=sems[1].at[step],
        device_id=partner, device_id_type=MESH)


def place_of(nz):
    r, c = lax.axis_index("row"), lax.axis_index("col")
    z, k = c // 2, lax.rem(c, 2)
    return r, c, z, k, [(r, 2 * lax.rem(z + step, nz) + k) for step in range(1, nz)]


def first_kernel(nz, count, source, got, send, recv):
    r, c, z, k, others = place_of(nz)
    greet(others)
    copies = [send_to(source.at[to[1] // 2, pl.ds(0, count)], got.at[z], (send, recv), step, to)
              for step, to in enumerate(others)]
    for copy in copies:
        copy.start()
    for copy in copies:
        copy.wait()


def second_kernel(n_row, nz, skip, source, wanted, got, plane_got, send, recv, psend, precv):
    r, c, z, k, others = place_of(nz)
    lines = [(lax.rem(r + step, n_row), c) for step in range(1, n_row)]
    greet(others + lines)
    count = got.shape[1]
    copies = [send_to(wanted.at[to[0]], plane_got.at[r], (psend, precv), step, to) for step, to in enumerate(lines)]
    copies += [send_to(source.at[to[1] // 2, pl.ds(skip, count)], got.at[z], (send, recv), step, to)
               for step, to in enumerate(others)]
    for copy in copies:
        copy.start()
    for copy in copies:
        copy.wait()


def left_kernel(nz, piece, got, send, recv, psend, precv):
    r, c, z, k, others = place_of(nz)
    mate = (r, 2 * z + 1 - k)
    greet(others + [mate])
    copies = [send_to(piece, got.at[c], (send, recv), step, to) for step, to in enumerate(others)]
    for copy in copies:
        copy.start()
    pairs = [send_to(piece, got.at[c], (psend, precv), 0, mate)]
    pairs[0].start()
    for step in range(1, nz):
        copies[step - 1].wait_recv()
        origin = 2 * lax.rem(z - step + nz, nz) + k
        pairs.append(send_to(got.at[origin], got.at[origin], (psend, precv), step, mate))
        pairs[-1].start()
    for copy in copies:
        copy.wait_send()
    for pair in pairs:
        pair.wait()


def last_kernel(n_row, nz, wanted, filtered, plane_got, every, send, recv, up_send, up_recv, down_send, down_recv,
                psend, precv):
    r, c, z, k, others = place_of(nz)
    mate = (r, 2 * z + 1 - k)
    barrier = pltpu.get_barrier_semaphore()
    lines = [(lax.rem(r + step, n_row), c) for step in range(1, n_row)]
    above, below = (r, 2 * lax.rem(z + 1, nz) + k), (r, 2 * lax.rem(z + nz - 1, nz) + k)
    greet(lines + [above, below, mate])
    plane = [send_to(wanted.at[to[0]], plane_got.at[r], (send, recv), step, to) for step, to in enumerate(lines)]

    def up(step, own):
        block = every.at[2 * lax.rem(z - step + nz, nz) + k]
        return send_to(filtered if own else block, block, (up_send, up_recv), step, above)

    def down(step, own):
        block = every.at[2 * lax.rem(z + step, nz) + k]
        return send_to(filtered if own else block, block, (down_send, down_recv), step, below)

    def across(step, own):
        block = every.at[2 * lax.rem(z + step, nz) + k]
        return send_to(filtered if own else block, block, (psend, precv), step, mate)

    @pl.when(z < nz - 1)
    def _():
        up(0, True).start()

    @pl.when(z > 0)
    def _():
        down(0, True).start()

    across(0, True).start()
    for copy in plane:
        copy.start()
    for step in range(1, nz):
        @pl.when(z - step >= 0)
        def _():
            up(step - 1, False).wait_recv()
            across(nz - step, False).start()

        @pl.when((z - step >= 0) & (z < nz - 1))
        def _():
            up(step, False).start()

        @pl.when(z + step <= nz - 1)
        def _():
            down(step - 1, False).wait_recv()
            across(step, False).start()

        @pl.when((z + step <= nz - 1) & (z > 0))
        def _():
            down(step, False).start()
    for step in range(nz):
        @pl.when((z - step >= 0) & (z < nz - 1))
        def _():
            up(step, False).wait_send()

        @pl.when((z + step <= nz - 1) & (z > 0))
        def _():
            down(step, False).wait_send()
    for step in range(nz):
        across(step, False).wait()
    for copy in plane:
        copy.wait()


def pick(sources, index, dest, sem):
    start = 0
    for source in sources:
        stop = start + source.shape[0]

        @pl.when((index >= start) & (index < stop))
        def _(source=source, start=start):
            pltpu.make_async_copy(source.at[index - start], dest, sem).start()

        start = stop


def gather_kernel(index, *refs):
    sources, (out, sem) = refs[:-2], refs[-2:]
    start = pl.program_id(0) * out.shape[0]

    def begin(i, carry):
        pick(sources, index[start + i], out.at[i], sem)
        return carry

    lax.fori_loop(0, out.shape[0], begin, 0)
    pltpu.make_async_copy(out, out, sem).wait()


def flat(array):
    return array.reshape((-1,) + array.shape[-2:])


def gather(index, *sources):
    block = sources[0].shape[-2:]
    count = index.shape[0]
    chunk = max(n for n in range(1, min(count, 512) + 1) if count % n == 0)
    return pl.pallas_call(
        gather_kernel,
        grid=(count // chunk,),
        out_shape=jax.ShapeDtypeStruct((count,) + block, sources[0].dtype),
        in_specs=[SMEM] + [ANY] * len(sources), out_specs=pl.BlockSpec((chunk,) + block, lambda i: (i, 0, 0)),
        scratch_shapes=[DMA],
        compiler_params=pltpu.CompilerParams(vmem_limit_bytes=BIG),
    )(index, *[flat(source) for source in sources])


def square_kernel(left_at, right_at, slot, keep, lefts, own_left, rights, own_rights, out, a, b, acc, sems):
    count = out.shape[0]

    def begin(i, carry):
        pick((lefts, own_left), left_at[i], a.at[i], sems.at[0])
        pick((rights, own_rights), right_at[i], b.at[i], sems.at[1])
        return carry

    lax.fori_loop(0, count, begin, 0)
    acc[...] = jnp.zeros_like(acc)
    pltpu.make_async_copy(a, a, sems.at[0]).wait()
    pltpu.make_async_copy(b, b, sems.at[1]).wait()

    def multiply(q, carry):
        ids = [q * 4 + i for i in range(4)]
        terms = [jnp.dot(a[i], b[i], preferred_element_type=jnp.float32) for i in ids]
        for i, term in zip(ids, terms):
            acc[slot[i]] += term
        return carry

    lax.fori_loop(0, count // 4, multiply, 0)

    def write(i, carry):
        out[i] = (acc[i] * keep[i].astype(jnp.float32)).astype(out.dtype)
        return carry

    lax.fori_loop(0, count, write, 0)


def cubed_kernel(left_at, right_at, target, own_target, every, own, got1, send1, got2, send2, out, a, b, f, acc, sems):
    count = a.shape[0]
    windows = acc.shape[0]
    block = a.shape[-1]
    per_window = count // windows
    own_per_window = f.shape[0] // windows
    mine = pltpu.make_async_copy(own, f, sems.at[2])
    mine.start()

    def begin(i, carry):
        pick((every, own), left_at[i], a.at[i], sems.at[0])
        pick((got1, send1, got2, send2), right_at[i], b.at[i], sems.at[1])
        return carry

    lax.fori_loop(0, count, begin, 0)
    acc[...] = jnp.zeros_like(acc)
    mine.wait()
    for w in range(windows):
        def add(i, carry):
            e = w * own_per_window + i
            acc[w, own_target[e]] -= 1.5 * f[e].astype(jnp.float32)
            return carry

        lax.fori_loop(0, own_per_window, add, 0)
    pltpu.make_async_copy(a, a, sems.at[0]).wait()
    pltpu.make_async_copy(b, b, sems.at[1]).wait()
    for w in range(windows):
        def multiply(q, carry):
            ids = [w * per_window + q * 4 + i for i in range(4)]
            terms = [jnp.dot(a[i], b[i], preferred_element_type=jnp.float32) for i in ids]
            for i, term in zip(ids, terms):
                acc[w, target[i]] += term
            return carry

        lax.fori_loop(0, per_window // 4, multiply, 0)
    for w in range(windows):
        for j in range(acc.shape[1]):
            out[w * block:(w + 1) * block, j * block:(j + 1) * block] = (-2.0 * acc[w, j]).astype(out.dtype)


def running(mask):
    n = mask.shape[-1]
    before = (jnp.arange(n)[:, None] < jnp.arange(n)[None, :]).astype(jnp.bfloat16)
    lines = mask.reshape(-1, n).astype(jnp.bfloat16)
    return jnp.dot(lines, before, preferred_element_type=jnp.float32).astype(jnp.int32).reshape(mask.shape)


def local(owned_blocks, owned_rows, owned_cols, keep):
    n_row, n_col = lax.axis_size("row"), lax.axis_size("col")
    devices = n_row * n_col
    nz = n_col // 2
    r, c = lax.axis_index("row"), lax.axis_index("col")
    z, k = c // 2, lax.rem(c, 2)
    block = owned_blocks.shape[-1]
    dtype = owned_blocks.dtype
    slots = owned_rows.shape[0]
    per_band = slots // n_row
    windows, gcols = keep.shape
    nb = gcols * n_col
    size = slots * (1 + n_col)
    tall = -(-size // 1024) * 8
    one = (block, block)
    chips = devices // 2
    pool = 2 * slots
    i32 = jnp.int32

    packed = jnp.concatenate([owned_rows[:, None], owned_cols], axis=1).reshape(-1)
    meta = jnp.pad(packed, (0, tall * 128 - size)).reshape(tall, 128)
    meta_all, sibling = pl.pallas_call(
        functools.partial(spread_kernel, n_row, n_col),
        out_shape=(jax.ShapeDtypeStruct((devices, tall, 128), i32),
                   jax.ShapeDtypeStruct((slots, nz) + one, dtype)),
        in_specs=[ANY, ANY], out_specs=(ANY, ANY),
        scratch_shapes=[DMA((devices,)), DMA((devices,)), DMA, DMA],
        compiler_params=remote_params(0),
    )(meta, owned_blocks.reshape((slots, nz, 2) + one))
    me = r * n_col + c
    is_me = jnp.arange(devices)[:, None] == me
    labels = jnp.where(is_me, packed[None, :], meta_all.reshape(devices, -1)[:, :size])
    labels = labels.reshape(devices * slots, 1 + n_col)
    rows, cols = labels[:, 0], labels[:, 1:]
    slot_ids = jnp.arange(devices * slots, dtype=i32)
    every_row = jnp.arange(nb, dtype=i32)
    filled = rows < gcols * 2
    row_id = jnp.where(filled, gcols * (slot_ids // per_band % n_row + n_row * (rows // gcols)) + rows % gcols, nb)
    holder = jnp.sum(jnp.where(row_id[None, :] == every_row[:, None], slot_ids[None, :], 0), axis=1)
    row_cols = cols[holder]
    chip = holder // pool
    line, plane = chip // nz, chip % nz

    base = gcols * jnp.arange(n_col, dtype=i32)
    window = gcols * jnp.arange(n_row, dtype=i32)[:, None] + jnp.arange(windows, dtype=i32)[None, :]
    inner = base + row_cols[window]
    targets = base + row_cols[inner]
    is_window = jnp.any(window[:, :, None] == every_row, axis=1)
    is_inner = jnp.any(inner.reshape(n_row, -1, 1) == every_row, axis=1) & ~is_window
    is_target = jnp.any(targets.reshape(n_row, -1, 1) == every_row, axis=1) & ~is_inner & ~is_window
    urgent = jnp.any(is_window | is_inner, axis=0)
    wanted_row = urgent.astype(i32) + jnp.any(is_window | is_inner | is_target, axis=0).astype(i32)
    wanted = jnp.where(filled, wanted_row[jnp.minimum(row_id, nb - 1)], 0).reshape(chips, pool)
    urgent_count = (wanted == 2).sum(axis=1)
    place = jnp.where(wanted == 2, running(wanted == 2), urgent_count[:, None] + running(wanted == 1))
    place = jnp.where(wanted > 0, place, pool)
    spot = place.reshape(-1)[holder]
    on_line = line[None, :] == jnp.arange(n_row, dtype=i32)[:, None]

    def ranks(need):
        both = need[:, None, :] & on_line[None, :, :]
        rank = jnp.sum(jnp.where(both, running(both), 0), axis=1)
        return rank, both.sum(axis=2).max()

    rank_window, _ = ranks(is_window)
    rank_inner, most_inner = ranks(is_inner)

    def shares(early, limit):
        now = is_target & (spot < early)[None, :]
        rank_now, _ = ranks(now)
        now = now & (rank_now < limit)
        later = is_target & ~now
        rank_later, most_later = ranks(later)
        return now, rank_now, later, rank_later, most_later

    inner_mine = inner[r].reshape(-1)
    targets_mine = targets[r].reshape(-1)
    cols_mine = lax.dynamic_index_in_dim(row_cols, c, 1, keepdims=False)
    square_target = cols_mine[inner_mine].reshape(windows, n_col)
    same = square_target[:, :, None] == square_target[:, None, :]
    first = jnp.argmax(same, axis=2).astype(i32)
    square_slot = (first + n_col * jnp.arange(windows, dtype=i32)[:, None]).reshape(-1)
    kept = jnp.take_along_axis(keep, square_target, axis=1).reshape(-1)
    cubed_target = cols_mine[targets_mine]
    entries = windows * n_col

    def run(caps, share, number):
        early, late, most, limit, rest = caps
        now, rank_now, later, rank_later, _ = share if share is not None else shares(early, limit)
        cap = early + late
        mine = lax.dynamic_index_in_dim(place, r * nz + z, 0, keepdims=False)
        pick_slot = jnp.sum(
            jnp.where(mine[None, :] == jnp.arange(cap)[:, None], jnp.arange(pool, dtype=i32)[None, :], 0), axis=1)
        zs = jnp.arange(nz, dtype=i32)[:, None]
        at = pick_slot[None, :] % slots
        index = jnp.where(
            pick_slot[None, :] // slots == k, at * n_col + 2 * zs + k, slots * n_col + at * nz + zs)
        outgoing = gather(index.reshape(-1), owned_blocks, sibling).reshape((nz, cap) + one)
        got_early = pl.pallas_call(
            functools.partial(first_kernel, nz, early),
            out_shape=jax.ShapeDtypeStruct((nz, early) + one, dtype),
            in_specs=[ANY], out_specs=ANY,
            scratch_shapes=[DMA((nz,)), DMA((nz,))],
            compiler_params=remote_params(number),
        )(outgoing)
        is_early = spot < early
        held_at = jnp.where(
            plane == z, nz * cap + plane * cap + spot,
            jnp.where(is_early, plane * early + spot, nz * early + plane * late + spot - early))
        early_at = jnp.where(plane == z, nz * early + plane * cap + spot, plane * early + spot)

        def demand(need, rank, count, source_at):
            sending = need & (line == r)[None, :]
            chosen = sending[:, None, :] & (rank[:, None, :] == jnp.arange(count, dtype=i32)[None, :, None])
            return jnp.sum(jnp.where(chosen, source_at[None, None, :], 0), axis=2)

        now_all = is_window | is_inner | now
        now_rank = jnp.where(is_window, rank_window, jnp.where(is_inner, windows + rank_inner, windows + most + rank_now))
        cap1 = windows + most + limit
        send1 = gather(demand(now_all, now_rank, cap1, early_at).reshape(-1), got_early, outgoing)
        send1 = send1.reshape((n_row, cap1) + one)
        got_late, got1 = pl.pallas_call(
            functools.partial(second_kernel, n_row, nz, early),
            out_shape=(jax.ShapeDtypeStruct((nz, late) + one, dtype),
                       jax.ShapeDtypeStruct((n_row, cap1) + one, dtype)),
            in_specs=[ANY, ANY], out_specs=(ANY, ANY),
            scratch_shapes=[DMA((nz,)), DMA((nz,)), DMA((n_row,)), DMA((n_row,))],
            compiler_params=remote_params(number + 1),
        )(outgoing, send1)
        found1 = line * cap1 + now_rank[r] + jnp.where(line == r, n_row * cap1, 0)
        window_mine = gcols * r + jnp.arange(windows, dtype=i32)
        left_mine = gather(found1[window_mine], got1, send1)
        lefts = pl.pallas_call(
            functools.partial(left_kernel, nz),
            out_shape=jax.ShapeDtypeStruct((n_col, windows) + one, dtype),
            in_specs=[ANY], out_specs=ANY,
            scratch_shapes=[DMA((nz,))] * 4,
            compiler_params=remote_params(number + 2),
        )(left_mine)
        ws = jnp.arange(windows, dtype=i32)[:, None]
        gs = jnp.arange(n_col, dtype=i32)[None, :]
        left_at = jnp.where(gs == c, n_col * windows + ws, gs * windows + ws).reshape(-1)
        filtered = pl.pallas_call(
            square_kernel,
            out_shape=jax.ShapeDtypeStruct((entries,) + one, dtype),
            in_specs=[SMEM] * 4 + [ANY] * 4, out_specs=VMEM,
            scratch_shapes=[pltpu.VMEM((entries,) + one, dtype), pltpu.VMEM((entries,) + one, dtype),
                            pltpu.VMEM((entries,) + one, jnp.float32), DMA((2,))],
            compiler_params=pltpu.CompilerParams(vmem_limit_bytes=BIG),
        )(left_at, found1[inner_mine], square_slot, kept, flat(lefts), left_mine, flat(got1), flat(send1))
        later_at = demand(later, rank_later, rest, held_at)
        send2 = gather(later_at.reshape(-1), got_early, got_late, outgoing).reshape((n_row, rest) + one)
        got2, every = pl.pallas_call(
            functools.partial(last_kernel, n_row, nz),
            out_shape=(jax.ShapeDtypeStruct((n_row, rest) + one, dtype),
                       jax.ShapeDtypeStruct((n_col, entries) + one, dtype)),
            in_specs=[ANY, ANY], out_specs=(ANY, ANY),
            scratch_shapes=[DMA((n_row,)), DMA((n_row,))] + [DMA((nz,))] * 6,
            compiler_params=remote_params(number + 3),
        )(send2, filtered)
        found2 = jnp.where(
            now_all[r], found1,
            2 * n_row * cap1 + line * rest + rank_later[r] + jnp.where(line == r, n_row * rest, 0))
        place3 = ws[:, :, None] * n_col + gs[:, :, None]
        groups = jnp.arange(n_col, dtype=i32)[None, None, :]
        left_at = jnp.where(groups == c, n_col * entries + place3, groups * entries + place3).reshape(-1)
        count = windows * n_col * n_col
        return pl.pallas_call(
            cubed_kernel,
            out_shape=jax.ShapeDtypeStruct((windows * block, gcols * block), dtype),
            in_specs=[SMEM] * 4 + [ANY] * 6, out_specs=VMEM,
            scratch_shapes=[pltpu.VMEM((count,) + one, dtype), pltpu.VMEM((count,) + one, dtype),
                            pltpu.VMEM((entries,) + one, dtype),
                            pltpu.VMEM((windows, gcols) + one, jnp.float32), DMA((3,))],
            compiler_params=pltpu.CompilerParams(vmem_limit_bytes=BIG),
        )(left_at, found2[targets_mine], cubed_target, square_target.reshape(-1), flat(every), filtered,
          flat(got1), flat(send1), flat(got2), flat(send2))

    most_demand = windows * n_col * n_col
    early, limit = 7 * pool // 32, most_demand // 8
    small = (early, early, 10 * entries // 16, limit, 22 * most_demand // 128)
    middle = (early, 26 * pool // 64, 12 * entries // 16, limit, most_demand // 4)
    full = (pool, 1, entries, limit, min(most_demand, nb, n_col * slots))
    share = shares(early, limit)
    most_pool, most_urgent = (wanted > 0).sum(axis=1).max(), urgent_count.max()

    def fits(caps):
        return ((most_pool <= caps[0] + caps[1]) & (most_urgent <= caps[0])
                & (most_inner <= caps[2]) & (share[-1] <= caps[4]))

    choice = jnp.where(fits(small), 0, jnp.where(fits(middle), 1, 2))
    return lax.switch(
        choice, [lambda: run(small, share, 1), lambda: run(middle, share, 5), lambda: run(full, None, 9)])


def solution(mesh):
    placed = (
        P(("row", "col"), None, None, None),
        P(("row", "col")),
        P(("row", "col"), None),
        P("row", "col"),
    )
    return jax.shard_map(
        local, mesh=mesh, in_specs=placed, out_specs=P("row", "col"), check_vma=False
    )
```

time: 285 us -> 229 us (0.80)
  Pallas kernels: 251 us -> 187 us
  local copies, waits for them, and re-layouts: 17.8 us -> 26.5 us
  other arithmetic: 11.1 us -> 8.15 us
    pallas_call x3, Pallas kernels: 125 us -> 94.6 us  [the longest x1 50.2 us: run(): pl.pallas_call(functools.partial(second_kernel, n_row, nz, early), out_sh...]
    pallas_call x1, Pallas kernels: 64.5 us -> 43.3 us  [run(): pl.pallas_call(functools.partial(last_kernel, n_row, nz), out_shape=(jax....]
    pallas_call x1, Pallas kernels: 23 us -> 10.6 us  [run(): pl.pallas_call(cubed_kernel, out_shape=jax.ShapeDtypeStruct((windows * bl...]
    gather x0 -> x4, local copies, waits for them, and re-layouts: none -> 9.09 us  [the longest x2 6.93 us: local(): wanted_row[jnp.minimum(row_id, nb - 1)]]
    reduce_sum x6 -> x4, other arithmetic: 5.37 us -> 1.31 us  [the longest x2 1 us: demand(): return jnp.sum(jnp.where(chosen, source_at[None, None, :], 0), axis=2)]
where the time goes in v2:
time: 229 us; the launch traced here: 227 us
  Pallas kernels  187 us (82%)
  local copies, waits for them, and re-layouts  26.5 us (12%)
  other arithmetic  8.15 us (4%)
  between operations  4.87 us (2%)
    pallas_call x1, Pallas kernels, run(): pl.pallas_call(functools.partial(second_kernel, n_row, nz, early), out_sh...  50.2 us
    pallas_call x1, Pallas kernels, run(): pl.pallas_call(functools.partial(last_kernel, n_row, nz), out_shape=(jax....  43.3 us
    pallas_call x1, Pallas kernels, run(): pl.pallas_call(functools.partial(first_kernel, nz, early), out_shape=jax....  34.4 us
    pallas_call x4, Pallas kernels, gather(): pl.pallas_call(gather_kernel, grid=(count // chunk,), out_shape=jax.Shape...  19.7 us
    pallas_call x1, Pallas kernels, local(): pl.pallas_call(functools.partial(spread_kernel, n_row, n_col), out_shape=...  14.9 us
    pallas_call x1, Pallas kernels, run(): pl.pallas_call(cubed_kernel, out_shape=jax.ShapeDtypeStruct((windows * bl...  10.6 us
    pallas_call x1, Pallas kernels, run(): pl.pallas_call(functools.partial(left_kernel, nz), out_shape=jax.ShapeDty...  9.99 us
    gather x2, local copies, waits for them, and re-layouts, local(): wanted_row[jnp.minimum(row_id, nb - 1)]  6.93 us

profile of v2, /device:TPU:0, one launch (start us, length us, event | category | flops | bytes accessed | tf_op | source)
XLA Modules:
  0.0 227.4 jit_solution(12634795439752084942)
XLA Ops:
  0.5 0.7 pad_add_fusion
  2.0 14.9 %shard_map.49 = (s32[32,8,128]{2,1,0:T(8,128)}, bf16[32,4,128,128]{3,2,1,0:T(8,128)(2,1)}) custom-call(s32[8,128]{1,0:T(8,128)} %pad_bitcast_fusion.meta, bf16[32,4,2,128,128]{4,3,2,1,0:T(8,128)(2,1)} %bitcast.89), custom_call_target="tpu_custom_call" | custom-call | tf_op jit(solution)/shard_map/pallas_call | solution.py:329
  16.9 0.9 copy.20
  18.5 1.0 fusion.31
  20.2 0.7 gather_fusion.9
  22.1 0.7 gather_fusion.14
  22.9 0.7 gather_fusion.16
  23.7 0.7 iota_reduce_fusion
  25.6 6.9 %gather_fusion.12 = s32[1024]{0:T(1024)S(1)} fusion(s32[256]{0:T(256)S(1)} %convert_add_fusion, s32[1024]{0:T(1024)S(1)} %get-tuple-element.338), kind=kCustom, calls=%fused_computation.12 | custom fusion | bytes 12288 | tf_op jit(solution)/shard_map/gather | solution.py:360
  32.6 0.6 reduce_max.37
  36.1 1.3 gather_fusion.15
  37.6 1.4 gather_fusion.13
  39.5 0.6 reduce_max.38
  42.0 0.6 reduce_max.39
  44.1 181.3 %conditional.1 = (bf16[256,4096]{1,0:T(8,128)(2,1)S(1)}) conditional(s32[]{:T(128)} %clamp.3, (s32[]{:T(128)}, pred[4,256]{1,0:T(4,128)(4,1)S(1)}, pred[4,256]{1,0:T(4,128)(4,1)S(1)}, pred[4,256]{1,0:T(4,128)(4,1)S(1)}, s32[]{:T(128)}, /*index=5*/s32[256]{0:T(256)S(1)}, s32[4,256]{1,0:T(4,128)S(1)}, s32[4,256]{1,0:T(4,128)S(1)}, ...), branch_computations={%region_18.23_spmd, %region_23.28_spmd, %region_28.34_spmd} | conditional | flops 5067584 | bytes 279886 | solution.py:499
  44.4 0.7 select_n.469.left_at
  45.9 6.5 %branch_0_fun.10.refs_1_.refs_2_ = bf16[112,128,128]{2,1,0:T(8,128)(2,1)} custom-call(s32[112]{0:T(128)} %select_n.465.index, bf16[256,128,128]{2,1,0:T(8,128)(2,1)} %bitcast.90, bf16[128,128,128]{2,1,0:T(8,128)(2,1)} %bitcast.105), custom_call_target="tpu_custom_call" | custom-call | tf_op jit(solution)/shard_map/cond/branch_0_fun/pallas_call | solution.py:222
  52.5 0.7 select_n.448.left_at
  53.3 1.2 gather_fusion.1
  54.5 1.2 gather_fusion.2
  55.7 1.8 gather_fusion
  59.8 34.4 %branch_0_fun.11 = bf16[4,14,128,128]{3,2,1,0:T(8,128)(2,1)} custom-call(bf16[4,28,128,128]{3,2,1,0:T(8,128)(2,1)} %bitcast.98), custom_call_target="tpu_custom_call" | custom-call | tf_op jit(solution)/shard_map/cond/branch_0_fun/pallas_call | solution.py:406
  94.2 5.3 %branch_0_fun.12.refs_1_.own_rights.send1 = bf16[112,128,128]{2,1,0:T(8,128)(2,1)} custom-call(s32[112]{0:T(128)} %reshape.1216.index, bf16[56,128,128]{2,1,0:T(8,128)(2,1)} %bitcast.117, bf16[112,128,128]{2,1,0:T(8,128)(2,1)} %branch_0_fun.10.refs_1_.refs_2_), custom_call_target="tpu_custom_call" | custom-call | tf_op jit(solution)/shard_map/cond/branch_0_fun/pallas_call | solution.py:222
  99.5 50.2 %branch_0_fun.13 = (bf16[4,14,128,128]{3,2,1,0:T(8,128)(2,1)}, bf16[4,28,128,128]{3,2,1,0:T(8,128)(2,1)}) custom-call(bf16[4,28,128,128]{3,2,1,0:T(8,128)(2,1)} %bitcast.99, bf16[4,28,128,128]{3,2,1,0:T(8,128)(2,1)} %bitcast.97), custom_call_target="tpu_custom_call" | custom-call | tf_op jit(solution)/shard_map/cond/branch_0_fun/pallas_call | solution.py:429
  149.7 5.9 %branch_0_fun.14.send2 = bf16[88,128,128]{2,1,0:T(8,128)(2,1)} custom-call(s32[88]{0:T(128)} %reshape.1211.index, bf16[56,128,128]{2,1,0:T(8,128)(2,1)} %bitcast.118, bf16[56,128,128]{2,1,0:T(8,128)(2,1)} %bitcast.130, bf16[112,128,128]{2,1,0:T(8,128)(2,1)} %branch_0_fun.10.refs_1_.refs_2_), custom_call_target="tpu_custom_call" | custom-call | tf_op jit(solution)/shard_map/cond/branch_0_fun/pallas_call | solution.py:222
  155.6 2.1 branch_0_fun.15.piece.own_left
  157.7 10.0 %branch_0_fun.16 = bf16[8,2,128,128]{3,2,1,0:T(8,128)(2,1)} custom-call(bf16[2,128,128]{2,1,0:T(8,128)(2,1)} %branch_0_fun.15.piece.own_left), custom_call_target="tpu_custom_call" | custom-call | tf_op jit(solution)/shard_map/cond/branch_0_fun/pallas_call | solution.py:440
  167.7 3.6 %branch_0_fun.17.filtered.own = bf16[16,128,128]{2,1,0:T(8,128)(2,1)} custom-call(s32[16]{0:T(128)} %select_n.469.left_at, s32[16]{0:T(128)} %gather_fusion.1, s32[16]{0:T(128)S(1)} %get-tuple-element.199.slot, s32[16]{0:T(128)S(1)} %get-tuple-element.200.keep, bf16[16,128,128]{2,1,0:T(8,128)(2,1)} %bitcast.127, ...), custom_call_target="tpu_custom_call" | custom-call | tf_op jit(solution)/shard_map/cond/branch_0_fun/pallas_call | solution.py:450
  171.3 43.3 %branch_0_fun.18 = (bf16[4,22,128,128]{3,2,1,0:T(8,128)(2,1)}, bf16[8,16,128,128]{3,2,1,0:T(8,128)(2,1)}) custom-call(bf16[4,22,128,128]{3,2,1,0:T(8,128)(2,1)} %bitcast.115, bf16[16,128,128]{2,1,0:T(8,128)(2,1)} %branch_0_fun.17.filtered.own), custom_call_target="tpu_custom_call" | custom-call | tf_op jit(solution)/shard_map/cond/branch_0_fun/pallas_call | solution.py:460
  214.6 10.6 %branch_0_fun.19 = bf16[256,4096]{1,0:T(8,128)(2,1)S(1)} custom-call(s32[128]{0:T(128)} %select_n.448.left_at, s32[128]{0:T(128)} %gather_fusion, s32[128]{0:T(128)S(1)} %get-tuple-element.187.target, s32[16]{0:T(128)S(1)} %get-tuple-element.188.own_target, bf16[128,128,128]{2,1,0:T(8,128)(2,1)} %bitcast.121, ...), custom_call_target="tpu_custom_call" | custom-call | tf_op jit(solution)/shard_map/cond/branch_0_fun/pallas_call | solution.py:475
  225.4 1.3 copy-done.2
  226.7 0.7 copy-done.1
  (125 shorter events, 11.1 us)
Async XLA Ops:
  0.0 22.9 %copy-start = (s32[2,32]{1,0:T(2,128)S(1)}, s32[2,32]{1,0:T(2,128)}, u32[]{:S(2)}) copy-start(s32[2,32]{1,0:T(2,128)} %param.10) | copy-start | bytes 772
  225.4 1.3 copy-start.2
  226.7 0.7 copy-start.1

commit v3 on v2

--- a/solution.py
+++ b/solution.py
@@ -88,13 +88,13 @@
         copy.wait()
 
 
-def second_kernel(n_row, nz, skip, source, wanted, got, plane_got, send, recv, psend, precv):
+def second_kernel(n_row, nz, source, wanted, got, plane_got, send, recv, psend, precv):
     r, c, z, k, others = place_of(nz)
     lines = [(lax.rem(r + step, n_row), c) for step in range(1, n_row)]
     greet(others + lines)
     count = got.shape[1]
     copies = [send_to(wanted.at[to[0]], plane_got.at[r], (psend, precv), step, to) for step, to in enumerate(lines)]
-    copies += [send_to(source.at[to[1] // 2, pl.ds(skip, count)], got.at[z], (send, recv), step, to)
+    copies += [send_to(source.at[to[1] // 2, pl.ds(0, count)], got.at[z], (send, recv), step, to)
                for step, to in enumerate(others)]
     for copy in copies:
         copy.start()
@@ -126,7 +126,6 @@
                 psend, precv):
     r, c, z, k, others = place_of(nz)
     mate = (r, 2 * z + 1 - k)
-    barrier = pltpu.get_barrier_semaphore()
     lines = [(lax.rem(r + step, n_row), c) for step in range(1, n_row)]
     above, below = (r, 2 * lax.rem(z + 1, nz) + k), (r, 2 * lax.rem(z + nz - 1, nz) + k)
     greet(lines + [above, below, mate])
@@ -357,7 +356,7 @@
     is_target = jnp.any(targets.reshape(n_row, -1, 1) == every_row, axis=1) & ~is_inner & ~is_window
     urgent = jnp.any(is_window | is_inner, axis=0)
     wanted_row = urgent.astype(i32) + jnp.any(is_window | is_inner | is_target, axis=0).astype(i32)
-    wanted = jnp.where(filled, wanted_row[jnp.minimum(row_id, nb - 1)], 0).reshape(chips, pool)
+    wanted = jnp.sum(jnp.where(row_id[:, None] == every_row[None, :], wanted_row[None, :], 0), axis=1).reshape(chips, pool)
     urgent_count = (wanted == 2).sum(axis=1)
     place = jnp.where(wanted == 2, running(wanted == 2), urgent_count[:, None] + running(wanted == 1))
     place = jnp.where(wanted > 0, place, pool)
@@ -391,50 +390,47 @@
     cubed_target = cols_mine[targets_mine]
     entries = windows * n_col
 
-    def run(caps, share, number):
-        early, late, most, limit, rest = caps
-        now, rank_now, later, rank_later, _ = share if share is not None else shares(early, limit)
-        cap = early + late
-        mine = lax.dynamic_index_in_dim(place, r * nz + z, 0, keepdims=False)
+    step = (z - plane + nz) % nz
+    zs = jnp.arange(nz, dtype=i32)[:, None]
+    place_mine = lax.dynamic_index_in_dim(place, r * nz + z, 0, keepdims=False)
+
+    def pooled(start, count):
+        position = start + jnp.arange(count, dtype=i32)
         pick_slot = jnp.sum(
-            jnp.where(mine[None, :] == jnp.arange(cap)[:, None], jnp.arange(pool, dtype=i32)[None, :], 0), axis=1)
-        zs = jnp.arange(nz, dtype=i32)[:, None]
+            jnp.where(place_mine[None, :] == position[:, None], jnp.arange(pool, dtype=i32)[None, :], 0), axis=1)
         at = pick_slot[None, :] % slots
         index = jnp.where(
             pick_slot[None, :] // slots == k, at * n_col + 2 * zs + k, slots * n_col + at * nz + zs)
-        outgoing = gather(index.reshape(-1), owned_blocks, sibling).reshape((nz, cap) + one)
-        got_early = pl.pallas_call(
-            functools.partial(first_kernel, nz, early),
-            out_shape=jax.ShapeDtypeStruct((nz, early) + one, dtype),
-            in_specs=[ANY], out_specs=ANY,
-            scratch_shapes=[DMA((nz,)), DMA((nz,))],
-            compiler_params=remote_params(number),
-        )(outgoing)
-        is_early = spot < early
-        held_at = jnp.where(
-            plane == z, nz * cap + plane * cap + spot,
-            jnp.where(is_early, plane * early + spot, nz * early + plane * late + spot - early))
-        early_at = jnp.where(plane == z, nz * early + plane * cap + spot, plane * early + spot)
-
-        def demand(need, rank, count, source_at):
-            sending = need & (line == r)[None, :]
-            chosen = sending[:, None, :] & (rank[:, None, :] == jnp.arange(count, dtype=i32)[None, :, None])
-            return jnp.sum(jnp.where(chosen, source_at[None, None, :], 0), axis=2)
-
+        return gather(index.reshape(-1), owned_blocks, sibling).reshape((nz, count) + one)
+
+    def demand(need, rank, count, source_at):
+        sending = need & (line == r)[None, :]
+        chosen = sending[:, None, :] & (rank[:, None, :] == jnp.arange(count, dtype=i32)[None, :, None])
+        return jnp.sum(jnp.where(chosen, source_at[None, None, :], 0), axis=2)
+
+    def opening(early, most, limit, share, parts):
+        now, rank_now = share[:2]
+        cap1 = windows + most + limit
         now_all = is_window | is_inner | now
         now_rank = jnp.where(is_window, rank_window, jnp.where(is_inner, windows + rank_inner, windows + most + rank_now))
-        cap1 = windows + most + limit
-        send1 = gather(demand(now_all, now_rank, cap1, early_at).reshape(-1), got_early, outgoing)
-        send1 = send1.reshape((n_row, cap1) + one)
+        send1 = gather(demand(now_all, now_rank, cap1, step * early + spot).reshape(-1), *parts)
+        found1 = line * cap1 + now_rank[r] + jnp.where(line == r, n_row * cap1, 0)
+        return now_all, found1, send1.reshape((n_row, cap1) + one)
+
+    def run(early, late, rest, share, parts, opened, outgoing, number):
+        later, rank_later = share[2:4]
+        now_all, found1, send1 = opened
+        cap1 = send1.shape[1]
+        late_at = jnp.where(plane == z, nz * late + plane * outgoing.shape[1], plane * late)
+        held_at = jnp.where(spot < early, step * early + spot, nz * early + late_at + spot - early)
         got_late, got1 = pl.pallas_call(
-            functools.partial(second_kernel, n_row, nz, early),
+            functools.partial(second_kernel, n_row, nz),
             out_shape=(jax.ShapeDtypeStruct((nz, late) + one, dtype),
                        jax.ShapeDtypeStruct((n_row, cap1) + one, dtype)),
             in_specs=[ANY, ANY], out_specs=(ANY, ANY),
             scratch_shapes=[DMA((nz,)), DMA((nz,)), DMA((n_row,)), DMA((n_row,))],
             compiler_params=remote_params(number + 1),
         )(outgoing, send1)
-        found1 = line * cap1 + now_rank[r] + jnp.where(line == r, n_row * cap1, 0)
         window_mine = gcols * r + jnp.arange(windows, dtype=i32)
         left_mine = gather(found1[window_mine], got1, send1)
         lefts = pl.pallas_call(
@@ -456,7 +452,7 @@
             compiler_params=pltpu.CompilerParams(vmem_limit_bytes=BIG),
         )(left_at, found1[inner_mine], square_slot, kept, flat(lefts), left_mine, flat(got1), flat(send1))
         later_at = demand(later, rank_later, rest, held_at)
-        send2 = gather(later_at.reshape(-1), got_early, got_late, outgoing).reshape((n_row, rest) + one)
+        send2 = gather(later_at.reshape(-1), *parts, got_late, outgoing).reshape((n_row, rest) + one)
         got2, every = pl.pallas_call(
             functools.partial(last_kernel, n_row, nz),
             out_shape=(jax.ShapeDtypeStruct((n_row, rest) + one, dtype),
@@ -484,20 +480,43 @@
           flat(got1), flat(send1), flat(got2), flat(send2))
 
     most_demand = windows * n_col * n_col
-    early, limit = 7 * pool // 32, most_demand // 8
-    small = (early, early, 10 * entries // 16, limit, 22 * most_demand // 128)
-    middle = (early, 26 * pool // 64, 12 * entries // 16, limit, most_demand // 4)
-    full = (pool, 1, entries, limit, min(most_demand, nb, n_col * slots))
+    early, most, limit = 7 * pool // 32, 10 * entries // 16, most_demand // 8
+    small = (early, 22 * most_demand // 128)
+    middle = (26 * pool // 64, most_demand // 4)
     share = shares(early, limit)
     most_pool, most_urgent = (wanted > 0).sum(axis=1).max(), urgent_count.max()
+    first_out = pooled(0, early)
+    parts = [lax.dynamic_index_in_dim(first_out, z, 0, keepdims=False)]
+    for by in range(1, nz):
+        moved = lax.dynamic_index_in_dim(first_out, (z + by) % nz, 0, keepdims=False)
+        parts.append(lax.ppermute(moved, "col", [(i, (i + 2 * by) % n_col) for i in range(n_col)]))
+    late_out = pooled(early, middle[0])
+    opened = opening(early, most, limit, share, parts)
+
+    def usual(caps, number):
+        return run(early, caps[0], caps[1], share, parts, opened, late_out, number)
+
+    def widest(number):
+        every_share = shares(pool, limit)
+        outgoing = pooled(0, pool)
+        got = pl.pallas_call(
+            functools.partial(first_kernel, nz, pool),
+            out_shape=jax.ShapeDtypeStruct((nz, pool) + one, dtype),
+            in_specs=[ANY], out_specs=ANY,
+            scratch_shapes=[DMA((nz,)), DMA((nz,))],
+            compiler_params=remote_params(number),
+        )(outgoing)
+        held = [lax.dynamic_index_in_dim(outgoing, z, 0, keepdims=False)]
+        held += [lax.dynamic_index_in_dim(got, (z - by + nz) % nz, 0, keepdims=False) for by in range(1, nz)]
+        return run(pool, 1, min(most_demand, nb, n_col * slots), every_share, held,
+                   opening(pool, entries, limit, every_share, held), outgoing, number)
 
     def fits(caps):
-        return ((most_pool <= caps[0] + caps[1]) & (most_urgent <= caps[0])
-                & (most_inner <= caps[2]) & (share[-1] <= caps[4]))
+        return ((most_pool <= early + caps[0]) & (most_urgent <= early)
+                & (most_inner <= most) & (share[-1] <= caps[1]))
 
     choice = jnp.where(fits(small), 0, jnp.where(fits(middle), 1, 2))
-    return lax.switch(
-        choice, [lambda: run(small, share, 1), lambda: run(middle, share, 5), lambda: run(full, None, 9)])
+    return lax.switch(choice, [lambda: usual(small, 1), lambda: usual(middle, 5), lambda: widest(9)])
 
 
 def solution(mesh):

time: 229 us -> 207 us (0.904)
  Pallas kernels: 187 us -> 146 us
  waiting for transfers between devices: 0 us -> 19.3 us
  local copies, waits for them, and re-layouts: 26.5 us -> 23.7 us
  starting transfers between devices: 0 us -> 2.38 us
    pallas_call x2 -> x1, Pallas kernels: 84.6 us -> 43.1 us  [run(): pl.pallas_call(functools.partial(second_kernel, n_row, nz), out_shape=(ja...]
    ppermute x0 -> x3, waiting for transfers between devices: none -> 19.3 us  [local(): lax.ppermute(moved, 'col', [(i, (i + 2 * by) % n_col) for i in range(n_co...]
    gather x2 -> x0, local copies, waits for them, and re-layouts: 6.93 us -> none  [local(): wanted_row[jnp.minimum(row_id, nb - 1)]]
    squeeze x0 -> x1, local copies, waits for them, and re-layouts: none -> 2.76 us  [local(): lax.dynamic_index_in_dim(first_out, (z + by) % nz, 0, keepdims=False)]
    ppermute x0 -> x3, starting transfers between devices: none -> 2.38 us  [local(): lax.ppermute(moved, 'col', [(i, (i + 2 * by) % n_col) for i in range(n_co...]
    pallas_call x4 -> x5, Pallas kernels: 19.7 us -> 21.2 us  [gather(): pl.pallas_call(gather_kernel, grid=(count // chunk,), out_shape=jax.Shape...]
  transfers between devices with their start and end apart: 0 -> 3, of which waited for: 0 -> 1; matrix products, arithmetic and copies ran while one was open for 0% -> 6% of each run, Pallas kernels for 0% -> 2%
where the time goes in v3:
time: 207 us; the launch traced here: 206 us
  Pallas kernels  146 us (71%)
  local copies, waits for them, and re-layouts  23.7 us (11%)
  waiting for transfers between devices  19.3 us (9%)
  other arithmetic  8.62 us (4%)
  between operations  4.25 us (2%)
  starting transfers between devices  2.38 us (1%)
    pallas_call x1, Pallas kernels, run(): pl.pallas_call(functools.partial(second_kernel, n_row, nz), out_shape=(ja...  43.1 us
    pallas_call x1, Pallas kernels, run(): pl.pallas_call(functools.partial(last_kernel, n_row, nz), out_shape=(jax....  42.9 us
    pallas_call x5, Pallas kernels, gather(): pl.pallas_call(gather_kernel, grid=(count // chunk,), out_shape=jax.Shape...  21.2 us
    ppermute x3, waiting for transfers between devices, local(): lax.ppermute(moved, 'col', [(i, (i + 2 * by) % n_col) for i in range(n_co...  19.3 us
    pallas_call x1, Pallas kernels, local(): pl.pallas_call(functools.partial(spread_kernel, n_row, n_col), out_shape=...  14.9 us
    pallas_call x1, Pallas kernels, run(): pl.pallas_call(cubed_kernel, out_shape=jax.ShapeDtypeStruct((windows * bl...  10.7 us
    pallas_call x1, Pallas kernels, run(): pl.pallas_call(functools.partial(left_kernel, nz), out_shape=jax.ShapeDty...  9.79 us
  transfers between devices with their start and end apart: 3, of which 1 were waited for; matrix products, arithmetic and copies ran while one was open for 6% of the time, Pallas kernels for 2%

profile of v3, /device:TPU:0, one launch (start us, length us, event | category | flops | bytes accessed | tf_op | source)
XLA Modules:
  0.0 205.6 jit_solution(9558692669081209544)
XLA Ops:
  0.1 0.7 pad_add_fusion
  1.6 14.9 %shard_map.49 = (s32[32,8,128]{2,1,0:T(8,128)}, bf16[32,4,128,128]{3,2,1,0:T(8,128)(2,1)}) custom-call(s32[8,128]{1,0:T(8,128)} %pad_bitcast_fusion.meta, bf16[32,4,2,128,128]{4,3,2,1,0:T(8,128)(2,1)} %bitcast.104), custom_call_target="tpu_custom_call" | custom-call | tf_op jit(solution)/shard_map/pallas_call | solution.py:328
  16.5 0.9 copy.18
  18.1 0.8 fusion.31
  19.7 0.7 gather_fusion.9
  23.4 0.7 select_n.695.index
  24.1 3.6 %shard_map.51 = bf16[56,128,128]{2,1,0:T(8,128)(2,1)} custom-call(s32[56]{0:T(128)} %select_n.695.index, bf16[256,128,128]{2,1,0:T(8,128)(2,1)} %bitcast.105, bf16[128,128,128]{2,1,0:T(8,128)(2,1)} %bitcast.114), custom_call_target="tpu_custom_call" | custom-call | tf_op jit(solution)/shard_map/pallas_call | solution.py:221
  27.7 2.8 %dynamic-slice_bitcast_fusion.4 = (bf16[14,128,128]{2,1,0:T(8,128)(2,1)}, bf16[14,128,128]{2,1,0:T(8,128)(2,1)}, bf16[14,128,128]{2,1,0:T(8,128)(2,1)}, bf16[14,128,128]{2,1,0:T(8,128)(2,1)}) fusion(bf16[4,14,128,128]{3,2,1,0:T(8,128)(2,1)} %bitcast.126, s32[]{:T(128)S(6)} %select_n.702, s32[]{:T(128)S(6)} %select_n.700, s32[]{:T(128)S(6)} %select_n.698, ...), kind=kLoop, calls=%fused_computation.202 | loop fusion | bytes 3670032 | tf_op jit(solution)/shard_map/jit(dynamic_index_in_dim)/squeeze | solution.py:491
  30.9 1.5 collective-permute-start.1
  33.2 0.7 gather_fusion.13
  34.2 0.7 iota_reduce_fusion
  35.0 1.4 gather_fusion.12
  38.7 0.7 reduce_max.37
  41.9 1.3 gather_fusion.14
  47.8 4.4 %shard_map.50 = bf16[104,128,128]{2,1,0:T(8,128)(2,1)S(1)} custom-call(s32[104]{0:T(128)} %select_n.687.index, bf16[256,128,128]{2,1,0:T(8,128)(2,1)} %bitcast.106, bf16[128,128,128]{2,1,0:T(8,128)(2,1)} %bitcast.115), custom_call_target="tpu_custom_call" | custom-call | tf_op jit(solution)/shard_map/pallas_call | solution.py:221
  52.2 0.7 gather_fusion.15
  53.6 19.3 %collective-permute-done.1.refs_2_ = bf16[14,128,128]{2,1,0:T(8,128)(2,1)} collective-permute-done((bf16[14,128,128]{2,1,0:T(8,128)(2,1)}, bf16[14,128,128]{2,1,0:T(8,128)(2,1)}, u32[]{:S(2)}, u32[]{:S(2)}) %collective-permute-start.1) | collective-permute-done | bytes 458784 | tf_op jit(solution)/shard_map/ppermute | solution.py:492
  72.9 5.4 %shard_map.52 = bf16[112,128,128]{2,1,0:T(8,128)(2,1)} custom-call(s32[112]{0:T(128)} %reshape.1376.index, bf16[14,128,128]{2,1,0:T(8,128)(2,1)} %get-tuple-element.577.refs_0_, bf16[14,128,128]{2,1,0:T(8,128)(2,1)} %collective-permute-done.refs_1_, bf16[14,128,128]{2,1,0:T(8,128)(2,1)} %collective-permute-done.1.refs_2_, ...), custom_call_target="tpu_custom_call" | custom-call | tf_op jit(solution)/shard_map/pallas_call | solution.py:221
  78.3 125.3 %conditional.1 = (bf16[256,4096]{1,0:T(8,128)(2,1)S(1)}) conditional(s32[]{:T(128)} %clamp.3, (s32[]{:T(128)}, pred[4,256]{1,0:T(4,128)(4,1)S(1)}, pred[4,256]{1,0:T(4,128)(4,1)S(1)}, s32[]{:T(128)}, s32[256]{0:T(256)S(1)}, /*index=5*/s32[4,256]{1,0:T(4,128)S(1)}, s32[4,256]{1,0:T(4,128)S(1)}, pred[4,256]{1,0:T(4,128)(4,1)S(1)}, ...), branch_computations={%region_22.25_spmd, %region_25.28_spmd, %region_28.34_spmd} | conditional | flops 5066372 | bytes 28433806 | solution.py:519
  78.5 0.8 select_n.546.left_at
  80.2 1.3 gather_fusion.1
  81.4 1.2 gather_fusion.2
  82.6 1.8 gather_fusion
  85.5 43.1 %branch_0_fun.11 = (bf16[4,14,128,128]{3,2,1,0:T(8,128)(2,1)}, bf16[4,28,128,128]{3,2,1,0:T(8,128)(2,1)}) custom-call(bf16[4,26,128,128]{3,2,1,0:T(8,128)(2,1)S(1)} %bitcast.109, bf16[4,28,128,128]{3,2,1,0:T(8,128)(2,1)} %bitcast.98), custom_call_target="tpu_custom_call" | custom-call | tf_op jit(solution)/shard_map/cond/branch_0_fun/pallas_call | solution.py:426
  128.6 5.7 %branch_0_fun.12.send2 = bf16[88,128,128]{2,1,0:T(8,128)(2,1)} custom-call(s32[88]{0:T(128)} %reshape.1319.index, bf16[14,128,128]{2,1,0:T(8,128)(2,1)} %get-tuple-element.434.refs_0_, bf16[14,128,128]{2,1,0:T(8,128)(2,1)} %get-tuple-element.435.refs_1_, bf16[14,128,128]{2,1,0:T(8,128)(2,1)} %get-tuple-element.436.refs_2_, ...), custom_call_target="tpu_custom_call" | custom-call | tf_op jit(solution)/shard_map/cond/branch_0_fun/pallas_call | solution.py:221
  134.4 2.1 %branch_0_fun.13.piece.own_left = bf16[2,128,128]{2,1,0:T(8,128)(2,1)} custom-call(s32[2]{0:T(128)} %gather_fusion.2, bf16[112,128,128]{2,1,0:T(8,128)(2,1)} %bitcast.118, bf16[112,128,128]{2,1,0:T(8,128)(2,1)S(1)} %copy-done.2), custom_call_target="tpu_custom_call" | custom-call | tf_op jit(solution)/shard_map/cond/branch_0_fun/pallas_call | solution.py:221
  136.4 9.8 %branch_0_fun.14 = bf16[8,2,128,128]{3,2,1,0:T(8,128)(2,1)} custom-call(bf16[2,128,128]{2,1,0:T(8,128)(2,1)} %branch_0_fun.13.piece.own_left), custom_call_target="tpu_custom_call" | custom-call | tf_op jit(solution)/shard_map/cond/branch_0_fun/pallas_call | solution.py:436
  146.2 3.6 %branch_0_fun.15.filtered.own = bf16[16,128,128]{2,1,0:T(8,128)(2,1)} custom-call(s32[16]{0:T(128)} %select_n.546.left_at, s32[16]{0:T(128)} %gather_fusion.1, s32[16]{0:T(128)S(1)} %get-tuple-element.442.slot, s32[16]{0:T(128)S(1)} %get-tuple-element.443.keep, bf16[16,128,128]{2,1,0:T(8,128)(2,1)} %bitcast.133, ...), custom_call_target="tpu_custom_call" | custom-call | tf_op jit(solution)/shard_map/cond/branch_0_fun/pallas_call | solution.py:446
  149.8 42.9 %branch_0_fun.16 = (bf16[4,22,128,128]{3,2,1,0:T(8,128)(2,1)}, bf16[8,16,128,128]{3,2,1,0:T(8,128)(2,1)}) custom-call(bf16[4,22,128,128]{3,2,1,0:T(8,128)(2,1)} %bitcast.124, bf16[16,128,128]{2,1,0:T(8,128)(2,1)} %branch_0_fun.15.filtered.own), custom_call_target="tpu_custom_call" | custom-call | tf_op jit(solution)/shard_map/cond/branch_0_fun/pallas_call | solution.py:456
  192.7 10.7 %branch_0_fun.17 = bf16[256,4096]{1,0:T(8,128)(2,1)S(1)} custom-call(s32[128]{0:T(128)} %select_n.533.left_at, s32[128]{0:T(128)} %gather_fusion, s32[128]{0:T(128)S(1)} %get-tuple-element.427.target, s32[16]{0:T(128)S(1)} %get-tuple-element.428.own_target, bf16[128,128,128]{2,1,0:T(8,128)(2,1)} %bitcast.128, ...), custom_call_target="tpu_custom_call" | custom-call | tf_op jit(solution)/shard_map/cond/branch_0_fun/pallas_call | solution.py:471
  203.6 1.3 copy-done.6
  205.0 0.7 copy-done.1
  (148 shorter events, 15.1 us)
Async XLA Ops:
  0.0 52.2 %copy-start = (s32[2,32]{1,0:T(2,128)S(1)}, s32[2,32]{1,0:T(2,128)}, u32[]{:S(2)}) copy-start(s32[2,32]{1,0:T(2,128)} %param.10) | copy-start | bytes 772
  23.2 13.2 %copy-start.7 = (s32[64]{0:T(128)}, s32[64]{0:T(128)S(1)}, u32[]{:S(2)}) copy-start(s32[64]{0:T(128)S(1)} %fusion.62) | copy-start | bytes 772
  30.5 23.1 %collective-permute-start.2 = (bf16[14,128,128]{2,1,0:T(8,128)(2,1)}, bf16[14,128,128]{2,1,0:T(8,128)(2,1)}, u32[]{:S(2)}, u32[]{:S(2)}) collective-permute-start(bf16[14,128,128]{2,1,0:T(8,128)(2,1)} %get-tuple-element.574), channel_id=1, source_target_pairs={{0,6},{1,7},{2,0},{3,1},{4,2},{5,3},{6,4},{7,5},{8,14},{9,15},{10,... | collective-permute-start | bytes 1376264 | tf_op jit(solution)/shard_map/ppermute | solution.py:492
  30.9 42.0 %collective-permute-start.1 = (bf16[14,128,128]{2,1,0:T(8,128)(2,1)}, bf16[14,128,128]{2,1,0:T(8,128)(2,1)}, u32[]{:S(2)}, u32[]{:S(2)}) collective-permute-start(bf16[14,128,128]{2,1,0:T(8,128)(2,1)} %get-tuple-element.575), channel_id=1, source_target_pairs={{0,4},{1,5},{2,6},{3,7},{4,0},{5,1},{6,2},{7,3},{8,12},{9,13},{10,... | collective-permute-start | bytes 1376264 | tf_op jit(solution)/shard_map/ppermute | solution.py:492
  32.3 40.6 %collective-permute-start = (bf16[14,128,128]{2,1,0:T(8,128)(2,1)}, bf16[14,128,128]{2,1,0:T(8,128)(2,1)}, u32[]{:S(2)}, u32[]{:S(2)}) collective-permute-start(bf16[14,128,128]{2,1,0:T(8,128)(2,1)} %get-tuple-element.576), channel_id=1, source_target_pairs={{0,2},{1,3},{2,4},{3,5},{4,6},{5,7},{6,0},{7,1},{8,10},{9,11},{10,... | collective-permute-start | bytes 1376264 | tf_op jit(solution)/shard_map/ppermute | solution.py:492
  78.3 50.3 %copy-start.4 = (bf16[104,128,128]{2,1,0:T(8,128)(2,1)}, bf16[104,128,128]{2,1,0:T(8,128)(2,1)S(1)}, u32[]{:S(2)}) copy-start(bf16[104,128,128]{2,1,0:T(8,128)(2,1)S(1)} %get-tuple-element.438.refs_5_) | copy-start | bytes 10223620 | tf_op jit(solution)/shard_map/cond
  128.6 5.7 %copy-start.2 = (bf16[112,128,128]{2,1,0:T(8,128)(2,1)S(1)}, bf16[112,128,128]{2,1,0:T(8,128)(2,1)}, u32[]{:S(2)}) copy-start(bf16[112,128,128]{2,1,0:T(8,128)(2,1)} %get-tuple-element.439.refs_1_.own_rights.send1) | copy-start | bytes 11010052 | tf_op jit(solution)/shard_map/cond
  203.6 1.3 copy-start.6
  205.0 0.7 copy-start.1
